TPU v7x, 512 devices: a whole 4x4x16 slice. The times are simulated.
512 devices in a mesh: dp: 16 (over z), row: 8 (over y, core), col: 4 (over x).
Axes of the slice: x: 4, y: 4, z: 16, core: 2. Of those that a mesh axis runs over, the one named last changes fastest.
Arguments:
- grad_blocks: bfloat16 [16, 4096, 1024], P('dp', 'row', 'col'), may hold values from -300 to 300
- ln_grads: bfloat16 [16, 4, 1024], P('dp', None, 'col'), may hold values from -240 to 240, as said below
- master: float32 [4096, 1024], P(('row', 'col')), may hold values from -6 to 6
- first_moment: float32 [4096, 1024], P(('row', 'col')), may hold values from -6 to 6
- second_moment: float32 [4096, 1024], P(('row', 'col')), may hold values from 0.3 to 3
- average: float32 [4096, 1024], P('row', 'col'), may hold values from -6 to 6
- ln_master: float32 [4, 1024], P(None, 'col'), may hold values from -6 to 6
- ln_first: float32 [4, 1024], P(None, 'col'), may hold values from -6 to 6
- ln_second: float32 [4, 1024], P(None, 'col'), may hold values from 0.3 to 3
- ln_average: float32 [4, 1024], P(None, 'col'), may hold values from -6 to 6
Outputs:
- average_new: float32 [4096, 1024], P('row', 'col')
- master_new: float32 [4096, 1024], P(('row', 'col'))
- first_new: float32 [4096, 1024], P(('row', 'col'))
- second_new: float32 [4096, 1024], P(('row', 'col'))
- ln_master_new: float32 [4, 1024], P(None, 'col')
- ln_first_new: float32 [4, 1024], P(None, 'col')
- ln_second_new: float32 [4, 1024], P(None, 'col')
- ln_average_new: float32 [4, 1024], P(None, 'col')
Inputs may be any that keep to these rules, and one draw needn't show every extreme that they name: `ln_grads`: partial gradients of each data-parallel group.
All inputs are finite; a program needn't handle non-finite values.
Results may differ from a plain program's by a relative error of at most 0.0003.
Values may be sent and summed in bfloat16 or wider, within the bound.
A program may use at most 64 MiB of HBM per device.

v0:
```python
import math

import jax
import jax.numpy as jnp
from jax import lax
from jax.sharding import PartitionSpec as P

D = 1024
FF = 4096
STEP = 20


beta_one = 0.9
beta_two = 0.95
learn_rate = 0.02
decay_rate = 0.1
epsilon = 1e-08
clip_rms = 1.0
ema_keep = 0.9


def adam_step(gradient, clip_scale, first, second, master, decay_weight):
    clipped = clip_scale * gradient
    first_new = beta_one * first + (1.0 - beta_one) * clipped
    second_new = beta_two * second + (1.0 - beta_two) * clipped * clipped
    direction = (
        first_new
        / (1.0 - beta_one**STEP)
        / (jnp.sqrt(second_new / (1.0 - beta_two**STEP)) + epsilon)
    )
    master_new = master - learn_rate * (direction + decay_weight * master)
    return (master_new, first_new, second_new)


def clip_factor(norm_total):
    return jnp.minimum(1.0, clip_rms * math.sqrt(FF * D + 4 * D) / jnp.sqrt(norm_total))


def squares(gradient, ln_gradient, row_count):
    return jnp.sum(gradient * gradient) + jnp.sum(ln_gradient * ln_gradient) / row_count


def shards(
    grad_blocks,
    ln_grads,
    master,
    first_moment,
    second_moment,
    average,
    ln_master,
    ln_first,
    ln_second,
    ln_average,
):
    row_count = float(lax.axis_size("row"))
    summed, ln_gradient = lax.psum(
        (grad_blocks[0].astype(jnp.float32), ln_grads[0].astype(jnp.float32)), "dp"
    )
    gradient = lax.all_to_all(summed, "col", split_axis=0, concat_axis=1, tiled=True)
    norm_total = lax.psum(squares(gradient, ln_gradient, row_count), ("row", "col"))
    clip_scale = clip_factor(norm_total)
    master_new, first_new, second_new = adam_step(
        gradient, clip_scale, first_moment, second_moment, master, decay_rate
    )
    ln_master_new, ln_first_new, ln_second_new = adam_step(
        ln_gradient, clip_scale, ln_first, ln_second, ln_master, 0.0
    )
    ln_average_new = ema_keep * ln_average + (1.0 - ema_keep) * ln_master_new
    block_master = lax.all_to_all(master_new, "col", split_axis=1, concat_axis=0, tiled=True)
    average_new = ema_keep * average + (1.0 - ema_keep) * block_master
    return (
        average_new,
        master_new,
        first_new,
        second_new,
        ln_master_new,
        ln_first_new,
        ln_second_new,
        ln_average_new,
    )


def solution(mesh):
    placed = (
        P("dp", "row", "col"),
        P("dp", None, "col"),
        P(("row", "col"), None),
        P(("row", "col"), None),
        P(("row", "col"), None),
        P("row", "col"),
        P(None, "col"),
        P(None, "col"),
        P(None, "col"),
        P(None, "col"),
    )
    return jax.shard_map(
        shards,
        mesh=mesh,
        in_specs=placed,
        out_specs=(
            P("row", "col"),
            P(("row", "col"), None),
            P(("row", "col"), None),
            P(("row", "col"), None),
            P(None, "col"),
            P(None, "col"),
            P(None, "col"),
            P(None, "col"),
        ),
        check_vma=False,
    )
```

profile of v0, /device:TPU:2, one launch (start us, length us, event | category | flops | bytes accessed | tf_op | source)
XLA Modules:
  0.0 162.7 jit_solution(14626310819225786435)
XLA Ops:
  0.6 0.7 bitcast_convert_fusion
  1.3 69.7 %all-reduce.2 = (f32[4,128,256]{2,1,0:T(8,128)}, f32[4,256]{1,0:T(4,128)S(1)}) all-reduce(bf16[4,128,256]{2,1,0:T(8,128)(2,1)} %bitcast.20, f32[4,256]{1,0:T(4,128)S(1)} %bitcast_convert_fusion), channel_id=1, replica_groups=mesh['dp'=16,'row'=8,'col'=4] {'dp'}, use_global_device_ids=true, to_apply=%region_0.0 | all-reduce | flops 132096 | bytes 794624 | tf_op jit(solution)/shard_map/psum | solution.py:56
  71.0 0.0 copy-start.1
  71.0 5.0 %all-to-all-start = ((f32[4,128,256]{2,1,0:T(8,128)}), f32[4,128,256]{2,1,0:T(8,128)S(1)}, u32[]{:S(2)}, u32[]{:S(2)}) async-start(f32[4,128,256]{2,1,0:T(8,128)} %get-tuple-element.16), calls=%async_computation | async-start | bytes 1048576 | tf_op jit(solution)/shard_map/all_to_all | solution.py:59
  76.0 0.0 copy-done.1
  76.0 0.0 copy-start.2
  76.0 0.2 copy.24
  76.2 0.8 copy-done.2
  77.0 0.2 copy.20
  77.2 0.0 copy-start.3
  77.2 0.6 multiply_reduce_fusion.1
  78.5 4.1 %all-to-all-done = f32[4,128,256]{2,1,0:T(8,128)S(1)} async-done(((f32[4,128,256]{2,1,0:T(8,128)}), f32[4,128,256]{2,1,0:T(8,128)S(1)}, u32[]{:S(2)}, u32[]{:S(2)}) %all-to-all-start) | async-done | bytes 524320 | tf_op jit(solution)/shard_map/all_to_all | solution.py:59
  82.6 0.7 multiply_reduce_fusion
  84.0 0.0 copy-done.3
  84.0 0.2 copy.22
  84.2 64.9 %psum.23 = f32[]{:T(128)} all-reduce(f32[]{:T(128)S(6)} %add.45), channel_id=1, replica_groups=mesh['dp'=16,'row'=8,'col'=4] {'row','col'}, use_global_device_ids=true, to_apply=%region_4.0 | all-reduce | flops 1 | bytes 8 | tf_op jit(solution)/shard_map/psum | solution.py:60
  149.8 0.2 copy.21
  150.0 0.4 multiply_subtract_fusion
  150.4 1.0 copy.25
  151.4 3.7 %all-to-all-start.1 = ((f32[128,4,256]{2,0,1:T(8,128)}), f32[128,4,256]{2,0,1:T(8,128)S(1)}, u32[]{:S(2)}, u32[]{:S(2)}) async-start(f32[128,4,256]{2,0,1:T(8,128)} %copy.25), calls=%async_computation.1 | async-start | bytes 1048576 | tf_op jit(solution)/shard_map/all_to_all | solution.py:69
  155.2 1.0 copy.26
  156.2 1.0 copy.27
  157.2 0.0 copy-start.4
  157.2 0.0 copy-start.5
  157.2 0.0 copy-start.6
  157.2 0.0 copy-start.7
  157.2 1.0 copy.28
  158.2 0.0 copy-done.4
  158.2 0.0 copy-done.5
  158.2 0.0 copy-done.6
  158.2 0.0 copy-done.7
  158.2 0.6 multiply_add_fusion
  158.8 0.0 copy-start
  158.8 3.0 %all-to-all-done.1 = f32[128,4,256]{2,0,1:T(8,128)S(1)} async-done(((f32[128,4,256]{2,0,1:T(8,128)}), f32[128,4,256]{2,0,1:T(8,128)S(1)}, u32[]{:S(2)}, u32[]{:S(2)}) %all-to-all-start.1) | async-done | bytes 524320 | tf_op jit(solution)/shard_map/all_to_all | solution.py:69
  161.9 0.0 copy-done
  161.9 0.9 bitcast_add_fusion
  (2 shorter events, 0.1 us)
Async XLA Ops:
  71.0 5.0 %copy-start.1 = (f32[128,1024]{1,0:T(8,128)S(1)}, f32[128,1024]{1,0:T(8,128)}, u32[]{:S(2)}) copy-start(f32[128,1024]{1,0:T(8,128)} %param.12) | copy-start | bytes 1572868
  71.0 11.6 %all-to-all-start = ((f32[4,128,256]{2,1,0:T(8,128)}), f32[4,128,256]{2,1,0:T(8,128)S(1)}, u32[]{:S(2)}, u32[]{:S(2)}) async-start(f32[4,128,256]{2,1,0:T(8,128)} %get-tuple-element.16), calls=%async_computation | async-start | bytes 1048576 | tf_op jit(solution)/shard_map/all_to_all | solution.py:59
  76.0 1.0 copy-start.2
  77.2 6.8 %copy-start.3 = (f32[128,1024]{1,0:T(8,128)S(1)}, f32[128,1024]{1,0:T(8,128)}, u32[]{:S(2)}) copy-start(f32[128,1024]{1,0:T(8,128)} %param.14) | copy-start | bytes 1572868
  151.4 10.4 %all-to-all-start.1 = ((f32[128,4,256]{2,0,1:T(8,128)}), f32[128,4,256]{2,0,1:T(8,128)S(1)}, u32[]{:S(2)}, u32[]{:S(2)}) async-start(f32[128,4,256]{2,0,1:T(8,128)} %copy.25), calls=%async_computation.1 | async-start | bytes 1048576 | tf_op jit(solution)/shard_map/all_to_all | solution.py:69
  157.2 1.0 copy-start.4
  157.2 1.0 copy-start.5
  157.2 1.0 copy-start.6
  157.2 1.0 copy-start.7
  158.8 3.0 %copy-start = (f32[512,256]{1,0:T(8,128)S(1)}, f32[512,256]{1,0:T(8,128)}, u32[]{:S(2)}) copy-start(f32[512,256]{1,0:T(8,128)} %param.15) | copy-start | bytes 1572868
where the time goes:
time: 163 us
  blocking collectives  135 us (83%)
  starting transfers between devices  8.69 us (5%)
  waiting for transfers between devices  7.11 us (4%)
  local copies, waits for them, and re-layouts  5.61 us (3%)
  other arithmetic  4.02 us (2%)
  between operations  2.72 us (2%)
    psum x1, blocking collectives, shards(): lax.psum((grad_blocks[0].astype(jnp.float32), ln_grads[0].astype(jnp.floa...  69.7 us
    psum x1, blocking collectives, shards(): lax.psum(squares(gradient, ln_gradient, row_count), ('row', 'col'))  64.9 us
    all_to_all x1, starting transfers between devices, shards(): lax.all_to_all(summed, 'col', split_axis=0, concat_axis=1, tiled=True)  4.96 us
    unnamed x22, local copies, waits for them, and re-layouts  4.42 us
    all_to_all x1, waiting for transfers between devices, shards(): lax.all_to_all(summed, 'col', split_axis=0, concat_axis=1, tiled=True)  4.12 us
    all_to_all x1, starting transfers between devices, shards(): lax.all_to_all(master_new, 'col', split_axis=1, concat_axis=0, tiled=True)  3.73 us
  transfers between devices with their start and end apart: 2, of which 2 were waited for; matrix products, arithmetic and copies ran while one was open for 3% of the time, Pallas kernels for 0%

commit v1 on v0

--- a/solution.py
+++ b/solution.py
@@ -1,9 +1,14 @@
+import functools
 import math
 
 import jax
 import jax.numpy as jnp
 from jax import lax
+from jax.experimental import pallas as pl
+from jax.experimental.pallas import tpu as pltpu
 from jax.sharding import PartitionSpec as P
+
+MESH = pl.DeviceIdType.MESH
 
 D = 1024
 FF = 4096
@@ -40,6 +45,65 @@
     return jnp.sum(gradient * gradient) + jnp.sum(ln_gradient * ln_gradient) / row_count
 
 
+def norm_kernel(n_row, n_col, x_ref, o_ref, buf, send_sem, recv_sem):
+    d = lax.axis_index("dp")
+    me = lax.axis_index("row") * n_col + lax.axis_index("col")
+    n = n_row * n_col
+    barrier = pltpu.get_barrier_semaphore()
+    for j in range(1, n):
+        peer = lax.rem(me + j, n)
+        pl.semaphore_signal(
+            barrier, inc=1, device_id=(d, peer // n_col, peer % n_col), device_id_type=MESH
+        )
+    pl.semaphore_wait(barrier, n - 1)
+    copies = []
+    for j in range(1, n):
+        peer = lax.rem(me + j, n)
+        copy = pltpu.make_async_remote_copy(
+            src_ref=x_ref,
+            dst_ref=buf.at[me],
+            send_sem=send_sem.at[j],
+            recv_sem=recv_sem.at[me],
+            device_id=(d, peer // n_col, peer % n_col),
+            device_id_type=MESH,
+        )
+        copy.start()
+        copies.append(copy)
+    buf[me] = x_ref[...]
+    for j in range(1, n):
+        sender = lax.rem(me + n - j, n)
+        pltpu.make_async_remote_copy(
+            src_ref=x_ref,
+            dst_ref=buf.at[sender],
+            send_sem=send_sem.at[j],
+            recv_sem=recv_sem.at[sender],
+            device_id=(d, sender // n_col, sender % n_col),
+            device_id_type=MESH,
+        ).wait_recv()
+    for copy in copies:
+        copy.wait_send()
+    o_ref[...] = jnp.sum(buf[...], axis=0)
+
+
+def group_sum(value):
+    n_row, n_col = lax.axis_size("row"), lax.axis_size("col")
+    n = n_row * n_col
+    tile = jnp.full((8, 128), value, jnp.float32)
+    out = pl.pallas_call(
+        functools.partial(norm_kernel, n_row, n_col),
+        out_shape=jax.ShapeDtypeStruct((8, 128), jnp.float32),
+        in_specs=[pl.BlockSpec(memory_space=pltpu.VMEM)],
+        out_specs=pl.BlockSpec(memory_space=pltpu.VMEM),
+        scratch_shapes=[
+            pltpu.VMEM((n, 8, 128), jnp.float32),
+            pltpu.SemaphoreType.DMA((n,)),
+            pltpu.SemaphoreType.DMA((n,)),
+        ],
+        compiler_params=pltpu.CompilerParams(collective_id=0, has_side_effects=True),
+    )(tile)
+    return out[0, 0]
+
+
 def shards(
     grad_blocks,
     ln_grads,
@@ -57,7 +121,7 @@
         (grad_blocks[0].astype(jnp.float32), ln_grads[0].astype(jnp.float32)), "dp"
     )
     gradient = lax.all_to_all(summed, "col", split_axis=0, concat_axis=1, tiled=True)
-    norm_total = lax.psum(squares(gradient, ln_gradient, row_count), ("row", "col"))
+    norm_total = group_sum(squares(gradient, ln_gradient, row_count))
     clip_scale = clip_factor(norm_total)
     master_new, first_new, second_new = adam_step(
         gradient, clip_scale, first_moment, second_moment, master, decay_rate

time: 163 us -> 116 us (0.71)
  the two profiles are of different devices: /device:TPU:2 before, /device:TPU:1 now
where the time goes in v1:
time: 116 us; the launch traced here: 115 us
  blocking collectives  56.8 us (49%)
  Pallas kernels  27.1 us (23%)
  waiting for transfers between devices  8.9 us (8%)
  local copies, waits for them, and re-layouts  8.24 us (7%)
  starting transfers between devices  7.62 us (7%)
  other arithmetic  4.02 us (3%)
  between operations  2.72 us (2%)
    psum x1, blocking collectives, shards(): lax.psum((grad_blocks[0].astype(jnp.float32), ln_grads[0].astype(jnp.floa...  56.8 us
    pallas_call x1, Pallas kernels, group_sum(): pl.pallas_call(functools.partial(norm_kernel, n_row, n_col), out_shape=ja...  27.1 us
    all_to_all x1, waiting for transfers between devices, shards(): lax.all_to_all(master_new, 'col', split_axis=1, concat_axis=0, tiled=True)  5.51 us
    unnamed x22, local copies, waits for them, and re-layouts  5.26 us
    all_to_all x1, starting transfers between devices, shards(): lax.all_to_all(summed, 'col', split_axis=0, concat_axis=1, tiled=True)  4.14 us
    all_to_all x1, starting transfers between devices, shards(): lax.all_to_all(master_new, 'col', split_axis=1, concat_axis=0, tiled=True)  3.47 us
    all_to_all x1, waiting for transfers between devices, shards(): lax.all_to_all(summed, 'col', split_axis=0, concat_axis=1, tiled=True)  3.39 us
  transfers between devices with their start and end apart: 2, of which 2 were waited for; matrix products, arithmetic and copies ran while one was open for 4% of the time, Pallas kernels for 0%

profile of v1, /device:TPU:1, one launch (start us, length us, event | category | flops | bytes accessed | tf_op | source)
XLA Modules:
  0.0 115.5 jit_solution(3091862033069751104)
XLA Ops:
  0.6 0.7 bitcast_convert_fusion
  1.3 56.8 %all-reduce.2 = (f32[4,128,256]{2,1,0:T(8,128)}, f32[4,256]{1,0:T(4,128)S(1)}) all-reduce(bf16[4,128,256]{2,1,0:T(8,128)(2,1)} %bitcast.21, f32[4,256]{1,0:T(4,128)S(1)} %bitcast_convert_fusion), channel_id=1, replica_groups=mesh['dp'=16,'row'=8,'col'=4] {'dp'}, use_global_device_ids=true, to_apply=%region_0.0 | all-reduce | flops 132096 | bytes 794624 | tf_op jit(solution)/shard_map/psum | solution.py:120
  58.1 0.0 copy-start.1
  58.1 4.1 %all-to-all-start = ((f32[4,128,256]{2,1,0:T(8,128)}), f32[4,128,256]{2,1,0:T(8,128)S(1)}, u32[]{:S(2)}, u32[]{:S(2)}) async-start(f32[4,128,256]{2,1,0:T(8,128)} %get-tuple-element.16), calls=%async_computation | async-start | bytes 1048576 | tf_op jit(solution)/shard_map/all_to_all | solution.py:123
  62.3 0.0 copy-done.1
  62.3 0.0 copy-start.2
  62.3 0.2 copy.24
  62.5 0.8 copy-done.2
  63.3 0.0 copy-start.3
  63.3 0.2 copy.20
  63.5 0.8 copy-done.3
  64.4 0.2 copy.22
  64.6 0.6 multiply_reduce_fusion.1
  65.8 3.4 %all-to-all-done = f32[4,128,256]{2,1,0:T(8,128)S(1)} async-done(((f32[4,128,256]{2,1,0:T(8,128)}), f32[4,128,256]{2,1,0:T(8,128)S(1)}, u32[]{:S(2)}, u32[]{:S(2)}) %all-to-all-start) | async-done | bytes 524320 | tf_op jit(solution)/shard_map/all_to_all | solution.py:123
  69.2 0.7 multiply_reduce_fusion
  70.6 0.6 broadcast_in_dim.3.x_ref
  71.2 27.1 %shard_map.161 = f32[8,128]{1,0:T(8,128)} custom-call(f32[8,128]{1,0:T(8,128)} %broadcast_in_dim.3.x_ref), custom_call_target="tpu_custom_call" | custom-call | tf_op jit(solution)/shard_map/pallas_call | solution.py:92
  98.4 1.2 %slice.3 = f32[1,1]{1,0:T(1,128)} slice(f32[8,128]{1,0:T(8,128)} %shard_map.161), slice={[0:1], [0:1]} | slice | bytes 8 | tf_op jit(solution)/shard_map/slice | solution.py:104
  100.2 0.2 copy.21
  100.5 0.4 multiply_subtract_fusion
  100.9 1.0 copy.25
  101.9 3.5 %all-to-all-start.1 = ((f32[128,4,256]{2,0,1:T(8,128)}), f32[128,4,256]{2,0,1:T(8,128)S(1)}, u32[]{:S(2)}, u32[]{:S(2)}) async-start(f32[128,4,256]{2,0,1:T(8,128)} %copy.25), calls=%async_computation.1 | async-start | bytes 1048576 | tf_op jit(solution)/shard_map/all_to_all | solution.py:133
  105.4 1.0 copy.26
  106.4 1.0 copy.27
  107.4 0.0 copy-start.4
  107.4 0.0 copy-start.5
  107.4 0.0 copy-start.6
  107.4 0.0 copy-start.7
  107.4 1.0 copy.28
  108.4 0.0 copy-done.4
  108.4 0.0 copy-done.5
  108.4 0.0 copy-done.6
  108.4 0.0 copy-done.7
  108.4 0.6 multiply_add_fusion
  109.0 0.0 copy-start
  109.0 5.5 %all-to-all-done.1 = f32[128,4,256]{2,0,1:T(8,128)S(1)} async-done(((f32[128,4,256]{2,0,1:T(8,128)}), f32[128,4,256]{2,0,1:T(8,128)S(1)}, u32[]{:S(2)}, u32[]{:S(2)}) %all-to-all-start.1) | async-done | bytes 524320 | tf_op jit(solution)/shard_map/all_to_all | solution.py:133
  114.6 0.0 copy-done
  114.6 0.9 bitcast_add_fusion
  (2 shorter events, 0.1 us)
Async XLA Ops:
  58.1 4.1 %copy-start.1 = (f32[128,1024]{1,0:T(8,128)S(1)}, f32[128,1024]{1,0:T(8,128)}, u32[]{:S(2)}) copy-start(f32[128,1024]{1,0:T(8,128)} %param.12) | copy-start | bytes 1572868
  58.1 11.1 %all-to-all-start = ((f32[4,128,256]{2,1,0:T(8,128)}), f32[4,128,256]{2,1,0:T(8,128)S(1)}, u32[]{:S(2)}, u32[]{:S(2)}) async-start(f32[4,128,256]{2,1,0:T(8,128)} %get-tuple-element.16), calls=%async_computation | async-start | bytes 1048576 | tf_op jit(solution)/shard_map/all_to_all | solution.py:123
  62.3 1.0 copy-start.2
  63.3 1.0 copy-start.3
  101.9 12.6 %all-to-all-start.1 = ((f32[128,4,256]{2,0,1:T(8,128)}), f32[128,4,256]{2,0,1:T(8,128)S(1)}, u32[]{:S(2)}, u32[]{:S(2)}) async-start(f32[128,4,256]{2,0,1:T(8,128)} %copy.25), calls=%async_computation.1 | async-start | bytes 1048576 | tf_op jit(solution)/shard_map/all_to_all | solution.py:133
  107.4 1.0 copy-start.4
  107.4 1.0 copy-start.5
  107.4 1.0 copy-start.6
  107.4 1.0 copy-start.7
  109.0 5.6 %copy-start = (f32[512,256]{1,0:T(8,128)S(1)}, f32[512,256]{1,0:T(8,128)}, u32[]{:S(2)}) copy-start(f32[512,256]{1,0:T(8,128)} %param.15) | copy-start | bytes 1572868

commit v2 on v1

--- a/solution.py
+++ b/solution.py
@@ -104,6 +104,171 @@
     return out[0, 0]
 
 
+def reduce_kernel(n_dp, n_col, g_ref, ln_ref, g_out, ln_out, rs_buf, ag_buf, ln_buf,
+                  rs_send, rs_recv, ag_send, ag_recv, ln_send, ln_recv):
+    d = lax.axis_index("dp")
+    r = lax.axis_index("row")
+    c = lax.axis_index("col")
+    n = n_dp * n_col
+    me = d * n_col + c
+    quarter = g_ref.shape[0] // n_col
+    depth = rs_buf.shape[2]
+    width = rs_buf.shape[3]
+    halves = g_ref.shape[1] // width
+    barrier = pltpu.get_barrier_semaphore()
+
+    def greet(j, carry):
+        peer = lax.rem(me + j, n)
+        pl.semaphore_signal(
+            barrier, inc=1, device_id=(peer // n_col, r, peer % n_col), device_id_type=MESH
+        )
+        return carry
+
+    lax.fori_loop(1, n, greet, 0)
+    pl.semaphore_wait(barrier, n - 1)
+
+    def piece(k, q):
+        rows = pl.ds(pl.multiple_of(q * quarter + (k // halves) * depth, depth), depth)
+        cols = pl.ds(pl.multiple_of((k % halves) * width, width), width)
+        return g_ref.at[rows, cols]
+
+    def rs_copy(j):
+        peer = lax.rem(me + j, n)
+        return pltpu.make_async_remote_copy(
+            src_ref=piece(peer // n_col, peer % n_col),
+            dst_ref=rs_buf.at[d, c],
+            send_sem=rs_send.at[j],
+            recv_sem=rs_recv.at[me],
+            device_id=(peer // n_col, r, peer % n_col),
+            device_id_type=MESH,
+        )
+
+    def ln_copy(j):
+        peer = lax.rem(d + j, n_dp)
+        return pltpu.make_async_remote_copy(
+            src_ref=ln_ref,
+            dst_ref=ln_buf.at[d],
+            send_sem=ln_send.at[j],
+            recv_sem=ln_recv.at[d],
+            device_id=(peer, r, c),
+            device_id_type=MESH,
+        )
+
+    def start_rs(j, carry):
+        rs_copy(j).start()
+        return carry
+
+    def start_ln(j, carry):
+        ln_copy(j).start()
+        return carry
+
+    lax.fori_loop(1, n, start_rs, 0)
+    lax.fori_loop(1, n_dp, start_ln, 0)
+    rs_buf[d, c] = piece(d, c)[...]
+    ln_buf[d] = ln_ref[...]
+
+    def wait_rs(j, carry):
+        src = lax.rem(me + j, n)
+        pltpu.make_async_remote_copy(
+            src_ref=piece(0, 0),
+            dst_ref=rs_buf.at[src // n_col, src % n_col],
+            send_sem=rs_send.at[j],
+            recv_sem=rs_recv.at[src],
+            device_id=(src // n_col, r, src % n_col),
+            device_id_type=MESH,
+        ).wait_recv()
+        rs_copy(j).wait_send()
+        return carry
+
+    lax.fori_loop(1, n, wait_rs, 0)
+    ag_buf[d] = jnp.sum(rs_buf[...].astype(jnp.float32), axis=0)
+
+    def ag_copy(j):
+        peer = lax.rem(d + j, n_dp)
+        return pltpu.make_async_remote_copy(
+            src_ref=ag_buf.at[d],
+            dst_ref=ag_buf.at[d],
+            send_sem=ag_send.at[j],
+            recv_sem=ag_recv.at[d],
+            device_id=(peer, r, c),
+            device_id_type=MESH,
+        )
+
+    def start_ag(j, carry):
+        ag_copy(j).start()
+        return carry
+
+    lax.fori_loop(1, n_dp, start_ag, 0)
+
+    def wait_ln(j, carry):
+        src = lax.rem(d + j, n_dp)
+        pltpu.make_async_remote_copy(
+            src_ref=ln_ref,
+            dst_ref=ln_buf.at[src],
+            send_sem=ln_send.at[j],
+            recv_sem=ln_recv.at[src],
+            device_id=(src, r, c),
+            device_id_type=MESH,
+        ).wait_recv()
+        ln_copy(j).wait_send()
+        return carry
+
+    lax.fori_loop(1, n_dp, wait_ln, 0)
+    ln_out[...] = jnp.sum(ln_buf[...].astype(jnp.float32), axis=0)
+
+    def wait_ag(j, carry):
+        src = lax.rem(d + j, n_dp)
+        pltpu.make_async_remote_copy(
+            src_ref=ag_buf.at[src],
+            dst_ref=ag_buf.at[src],
+            send_sem=ag_send.at[j],
+            recv_sem=ag_recv.at[src],
+            device_id=(src, r, c),
+            device_id_type=MESH,
+        ).wait_recv()
+        ag_copy(j).wait_send()
+        return carry
+
+    lax.fori_loop(1, n_dp, wait_ag, 0)
+    for k in range(n_dp):
+        for q in range(n_col):
+            g_out[
+                pl.ds((k // halves) * depth, depth),
+                pl.ds(q * halves * width + (k % halves) * width, width),
+            ] = ag_buf[k, q]
+
+
+def reduce_blocks(block, ln_part):
+    n_dp, n_col = lax.axis_size("dp"), lax.axis_size("col")
+    rows, cols = block.shape
+    quarter = rows // n_col
+    width = 128
+    halves = cols // width
+    depth = quarter * halves // n_dp
+    vmem = pl.BlockSpec(memory_space=pltpu.VMEM)
+    return pl.pallas_call(
+        functools.partial(reduce_kernel, n_dp, n_col),
+        out_shape=(
+            jax.ShapeDtypeStruct((quarter, cols * n_col), jnp.float32),
+            jax.ShapeDtypeStruct(ln_part.shape, jnp.float32),
+        ),
+        in_specs=[vmem, vmem],
+        out_specs=(vmem, vmem),
+        scratch_shapes=[
+            pltpu.VMEM((n_dp, n_col, depth, width), block.dtype),
+            pltpu.VMEM((n_dp, n_col, depth, width), jnp.float32),
+            pltpu.VMEM((n_dp,) + ln_part.shape, ln_part.dtype),
+            pltpu.SemaphoreType.DMA((n_dp * n_col,)),
+            pltpu.SemaphoreType.DMA((n_dp * n_col,)),
+            pltpu.SemaphoreType.DMA((n_dp,)),
+            pltpu.SemaphoreType.DMA((n_dp,)),
+            pltpu.SemaphoreType.DMA((n_dp,)),
+            pltpu.SemaphoreType.DMA((n_dp,)),
+        ],
+        compiler_params=pltpu.CompilerParams(collective_id=1, has_side_effects=True),
+    )(block, ln_part)
+
+
 def shards(
     grad_blocks,
     ln_grads,
@@ -117,10 +282,7 @@
     ln_average,
 ):
     row_count = float(lax.axis_size("row"))
-    summed, ln_gradient = lax.psum(
-        (grad_blocks[0].astype(jnp.float32), ln_grads[0].astype(jnp.float32)), "dp"
-    )
-    gradient = lax.all_to_all(summed, "col", split_axis=0, concat_axis=1, tiled=True)
+    gradient, ln_gradient = reduce_blocks(grad_blocks[0], ln_grads[0])
     norm_total = group_sum(squares(gradient, ln_gradient, row_count))
     clip_scale = clip_factor(norm_total)
     master_new, first_new, second_new = adam_step(

time: 116 us -> 97 us (0.84)
  blocking collectives: 56.8 us -> 0 us
  Pallas kernels: 27.1 us -> 71.6 us
  local copies, waits for them, and re-layouts: 8.24 us -> 2.78 us
  starting transfers between devices: 7.62 us -> 3.62 us
  other arithmetic: 4.02 us -> 7.38 us
    pallas_call x0 -> x1, Pallas kernels: none -> 57.4 us  [reduce_blocks(): pl.pallas_call(functools.partial(reduce_kernel, n_dp, n_col), out_shape=(...]
    psum x1 -> x0, blocking collectives: 56.8 us -> none  [shards(): lax.psum((grad_blocks[0].astype(jnp.float32), ln_grads[0].astype(jnp.floa...]
    pallas_call x1, Pallas kernels: 27.1 us -> 14.2 us  [group_sum(): pl.pallas_call(functools.partial(norm_kernel, n_row, n_col), out_shape=ja...]
    unnamed x22 -> x16, local copies, waits for them, and re-layouts: 5.26 us -> 0.09 us
    all_to_all x1 -> x0, starting transfers between devices: 4.14 us -> none  [shards(): lax.all_to_all(summed, 'col', split_axis=0, concat_axis=1, tiled=True)]
    all_to_all x1 -> x0, waiting for transfers between devices: 3.39 us -> none  [shards(): lax.all_to_all(summed, 'col', split_axis=0, concat_axis=1, tiled=True)]
    all_to_all x1, waiting for transfers between devices: 5.51 us -> 8.47 us  [shards(): lax.all_to_all(master_new, 'col', split_axis=1, concat_axis=0, tiled=True)]
    sub x1, other arithmetic: 0.42 us -> 2.73 us  [adam_step(): master_new = master - learn_rate * (direction + decay_weight * master)]
  transfers between devices with their start and end apart: 2 -> 1, of which waited for: 2 -> 1; matrix products, arithmetic and copies ran while one was open for 4% -> 1% of each run, Pallas kernels for 0% -> 0%
where the time goes in v2:
time: 97 us; the launch traced here: 96.6 us
  Pallas kernels  71.6 us (74%)
  waiting for transfers between devices  8.47 us (9%)
  other arithmetic  7.38 us (8%)
  starting transfers between devices  3.62 us (4%)
  local copies, waits for them, and re-layouts  2.78 us (3%)
  between operations  2.73 us (3%)
    pallas_call x1, Pallas kernels, reduce_blocks(): pl.pallas_call(functools.partial(reduce_kernel, n_dp, n_col), out_shape=(...  57.4 us
    pallas_call x1, Pallas kernels, group_sum(): pl.pallas_call(functools.partial(norm_kernel, n_row, n_col), out_shape=ja...  14.2 us
    all_to_all x1, waiting for transfers between devices, shards(): lax.all_to_all(master_new, 'col', split_axis=1, concat_axis=0, tiled=True)  8.47 us
    all_to_all x1, starting transfers between devices, shards(): lax.all_to_all(master_new, 'col', split_axis=1, concat_axis=0, tiled=True)  3.62 us
    sub x1, other arithmetic, adam_step(): master_new = master - learn_rate * (direction + decay_weight * master)  2.73 us
  transfers between devices with their start and end apart: 1, of which 1 were waited for; matrix products, arithmetic and copies ran while one was open for 1% of the time, Pallas kernels for 0%

profile of v2, /device:TPU:1, one launch (start us, length us, event | category | flops | bytes accessed | tf_op | source)
XLA Modules:
  0.0 96.6 jit_solution(17770265890913480158)
XLA Ops:
  0.6 57.4 %shard_map.161 = (f32[128,1024]{1,0:T(8,128)}, f32[4,256]{1,0:T(4,128)}) custom-call(bf16[512,256]{1,0:T(8,128)(2,1)} %bitcast.12, bf16[4,256]{1,0:T(4,128)(2,1)} %bitcast.13), custom_call_target="tpu_custom_call" | custom-call | tf_op jit(solution)/shard_map/pallas_call | solution.py:249
  58.0 0.0 copy-start.1
  58.0 1.3 %multiply_reduce_fusion.1 = f32[]{:T(128)} fusion(f32[4,256]{1,0:T(4,128)} %get-tuple-element.11), kind=kLoop, calls=%fused_computation.13 | loop fusion | flops 2047 | bytes 4100 | tf_op jit(solution)/shard_map/reduce_sum | solution.py:45
  59.3 1.8 %multiply_reduce_fusion = f32[]{:T(128)} fusion(f32[128,1024]{1,0:T(8,128)} %get-tuple-element.10), kind=kLoop, calls=%fused_computation.6 | loop fusion | flops 262143 | bytes 524292 | tf_op jit(solution)/shard_map/reduce_sum | solution.py:45
  62.4 0.6 broadcast_in_dim.3.x_ref
  63.0 14.2 %shard_map.162 = f32[8,128]{1,0:T(8,128)} custom-call(f32[8,128]{1,0:T(8,128)} %broadcast_in_dim.3.x_ref), custom_call_target="tpu_custom_call" | custom-call | tf_op jit(solution)/shard_map/pallas_call | solution.py:92
  77.3 1.2 %slice.3 = f32[1,1]{1,0:T(1,128)} slice(f32[8,128]{1,0:T(8,128)} %shard_map.162), slice={[0:1], [0:1]} | slice | bytes 8 | tf_op jit(solution)/shard_map/slice | solution.py:104
  79.1 0.0 copy-done.1
  79.2 2.7 %multiply_subtract_fusion = (f32[128,1024]{1,0:T(8,128)S(1)}, f32[128,1024]{1,0:T(8,128)}, f32[128,1024]{1,0:T(8,128)}) fusion(f32[128,1024]{1,0:T(8,128)} %param.12, f32[128,1024]{1,0:T(8,128)S(1)} %copy-done.1, f32[]{:T(128)} %bitcast.2, f32[128,1024]{1,0:T(8,128)} %param.13, f32[128,1024]{1,0:T(8,128)} %param.14), kind=kLoop, calls=%fused_computation.4 | loop fusion | flops 2097152 | bytes 3670020 | tf_op jit(solution)/shard_map/sub | solution.py:36
  81.9 0.0 copy-start
  81.9 0.9 copy.22
  82.8 0.1 copy-done
  82.9 0.0 copy-start.3
  82.9 0.0 copy-start.4
  82.9 0.0 copy-start.5
  82.9 0.0 copy-start.6
  82.9 0.0 copy-start.7
  82.9 3.6 %all-to-all-start = ((f32[128,4,256]{2,0,1:T(8,128)}), f32[128,4,256]{2,0,1:T(8,128)S(1)}, u32[]{:S(2)}, u32[]{:S(2)}) async-start(f32[128,4,256]{2,0,1:T(8,128)} %bitcast.10), calls=%async_computation | async-start | bytes 1048576 | tf_op jit(solution)/shard_map/all_to_all | solution.py:295
  86.5 0.0 copy-done.3
  86.5 0.0 copy-done.4
  86.5 0.0 copy-done.5
  86.5 0.0 copy-done.6
  86.5 0.0 copy-done.7
  86.5 0.6 multiply_add_fusion.1
  87.2 0.0 copy-start.2
  87.2 8.5 %all-to-all-done = f32[128,4,256]{2,0,1:T(8,128)S(1)} async-done(((f32[128,4,256]{2,0,1:T(8,128)}), f32[128,4,256]{2,0,1:T(8,128)S(1)}, u32[]{:S(2)}, u32[]{:S(2)}) %all-to-all-start) | async-done | bytes 524320 | tf_op jit(solution)/shard_map/all_to_all | solution.py:295
  95.7 0.0 copy-done.2
  95.7 0.9 bitcast_add_fusion
  (1 shorter events, 0.0 us)
Async XLA Ops:
  58.0 21.2 %copy-start.1 = (f32[128,1024]{1,0:T(8,128)S(1)}, f32[128,1024]{1,0:T(8,128)}, u32[]{:S(2)}) copy-start(f32[128,1024]{1,0:T(8,128)} %get-tuple-element.10) | copy-start | bytes 1572868
  81.9 1.0 copy-start
  82.9 3.6 %copy-start.3 = (f32[4,256]{1,0:T(4,128)S(1)}, f32[4,256]{1,0:T(4,128)}, u32[]{:S(2)}) copy-start(f32[4,256]{1,0:T(4,128)} %get-tuple-element.11) | copy-start | bytes 12292
  82.9 3.7 %copy-start.4 = (f32[4,256]{1,0:T(4,128)S(1)}, f32[4,256]{1,0:T(4,128)}, u32[]{:S(2)}) copy-start(f32[4,256]{1,0:T(4,128)} %param.19) | copy-start | bytes 12292
  82.9 3.7 %copy-start.5 = (f32[4,256]{1,0:T(4,128)S(1)}, f32[4,256]{1,0:T(4,128)}, u32[]{:S(2)}) copy-start(f32[4,256]{1,0:T(4,128)} %param.16) | copy-start | bytes 12292
  82.9 3.7 %copy-start.6 = (f32[4,256]{1,0:T(4,128)S(1)}, f32[4,256]{1,0:T(4,128)}, u32[]{:S(2)}) copy-start(f32[4,256]{1,0:T(4,128)} %param.17) | copy-start | bytes 12292
  82.9 3.7 %copy-start.7 = (f32[4,256]{1,0:T(4,128)S(1)}, f32[4,256]{1,0:T(4,128)}, u32[]{:S(2)}) copy-start(f32[4,256]{1,0:T(4,128)} %param.18) | copy-start | bytes 12292
  82.9 12.8 %all-to-all-start = ((f32[128,4,256]{2,0,1:T(8,128)}), f32[128,4,256]{2,0,1:T(8,128)S(1)}, u32[]{:S(2)}, u32[]{:S(2)}) async-start(f32[128,4,256]{2,0,1:T(8,128)} %bitcast.10), calls=%async_computation | async-start | bytes 1048576 | tf_op jit(solution)/shard_map/all_to_all | solution.py:295
  87.2 8.5 %copy-start.2 = (f32[512,256]{1,0:T(8,128)S(1)}, f32[512,256]{1,0:T(8,128)}, u32[]{:S(2)}) copy-start(f32[512,256]{1,0:T(8,128)} %param.15) | copy-start | bytes 1572868

commit v3 on v2

--- a/solution.py
+++ b/solution.py
@@ -105,7 +105,7 @@
 
 
 def reduce_kernel(n_dp, n_col, g_ref, ln_ref, g_out, ln_out, rs_buf, ag_buf, ln_buf,
-                  rs_send, rs_recv, ag_send, ag_recv, ln_send, ln_recv):
+                  rs_send, rs_recv, ag_send, ag_recv, ag_lsend, ag_lrecv, ln_send, ln_recv):
     d = lax.axis_index("dp")
     r = lax.axis_index("row")
     c = lax.axis_index("col")
@@ -183,22 +183,35 @@
     lax.fori_loop(1, n, wait_rs, 0)
     ag_buf[d] = jnp.sum(rs_buf[...].astype(jnp.float32), axis=0)
 
-    def ag_copy(j):
-        peer = lax.rem(d + j, n_dp)
+    def ring_copy(slot, step, toward, send_sem, recv_sem):
         return pltpu.make_async_remote_copy(
-            src_ref=ag_buf.at[d],
-            dst_ref=ag_buf.at[d],
-            send_sem=ag_send.at[j],
-            recv_sem=ag_recv.at[d],
-            device_id=(peer, r, c),
-            device_id_type=MESH,
-        )
-
-    def start_ag(j, carry):
-        ag_copy(j).start()
-        return carry
-
-    lax.fori_loop(1, n_dp, start_ag, 0)
+            src_ref=ag_buf.at[slot],
+            dst_ref=ag_buf.at[slot],
+            send_sem=send_sem.at[step],
+            recv_sem=recv_sem.at[slot],
+            device_id=(toward, r, c),
+            device_id_type=MESH,
+        )
+
+    right = lax.rem(d + 1, n_dp)
+    left = lax.rem(d + n_dp - 1, n_dp)
+    n_right = n_dp // 2
+    n_left = n_dp - 1 - n_right
+    sends = []
+    for step in range(1, n_right + 1):
+        slot = lax.rem(d + n_dp - step + 1, n_dp)
+        if step > 1:
+            ring_copy(slot, step, left, ag_send, ag_recv).wait_recv()
+        copy = ring_copy(slot, step, right, ag_send, ag_recv)
+        copy.start()
+        sends.append(copy)
+        if step <= n_left:
+            slot = lax.rem(d + step - 1, n_dp)
+            if step > 1:
+                ring_copy(slot, step, right, ag_lsend, ag_lrecv).wait_recv()
+            copy = ring_copy(slot, step, left, ag_lsend, ag_lrecv)
+            copy.start()
+            sends.append(copy)
 
     def wait_ln(j, carry):
         src = lax.rem(d + j, n_dp)
@@ -216,20 +229,10 @@
     lax.fori_loop(1, n_dp, wait_ln, 0)
     ln_out[...] = jnp.sum(ln_buf[...].astype(jnp.float32), axis=0)
 
-    def wait_ag(j, carry):
-        src = lax.rem(d + j, n_dp)
-        pltpu.make_async_remote_copy(
-            src_ref=ag_buf.at[src],
-            dst_ref=ag_buf.at[src],
-            send_sem=ag_send.at[j],
-            recv_sem=ag_recv.at[src],
-            device_id=(src, r, c),
-            device_id_type=MESH,
-        ).wait_recv()
-        ag_copy(j).wait_send()
-        return carry
-
-    lax.fori_loop(1, n_dp, wait_ag, 0)
+    ring_copy(lax.rem(d + n_dp - n_right, n_dp), 0, left, ag_send, ag_recv).wait_recv()
+    ring_copy(lax.rem(d + n_left, n_dp), 0, right, ag_lsend, ag_lrecv).wait_recv()
+    for copy in sends:
+        copy.wait_send()
     for k in range(n_dp):
         for q in range(n_col):
             g_out[
@@ -264,6 +267,8 @@
             pltpu.SemaphoreType.DMA((n_dp,)),
             pltpu.SemaphoreType.DMA((n_dp,)),
             pltpu.SemaphoreType.DMA((n_dp,)),
+            pltpu.SemaphoreType.DMA((n_dp,)),
+            pltpu.SemaphoreType.DMA((n_dp,)),
         ],
         compiler_params=pltpu.CompilerParams(collective_id=1, has_side_effects=True),
     )(block, ln_part)

time: 97 us -> 103 us (1.062)
  Pallas kernels: 71.6 us -> 77.2 us
    pallas_call x1, Pallas kernels: 14.2 us -> 22.8 us  [group_sum(): pl.pallas_call(functools.partial(norm_kernel, n_row, n_col), out_shape=ja...]
    pallas_call x1, Pallas kernels: 57.4 us -> 54.4 us  [reduce_blocks(): pl.pallas_call(functools.partial(reduce_kernel, n_dp, n_col), out_shape=(...]
where the time goes in v3:
time: 103 us; the launch traced here: 102 us
  Pallas kernels  77.2 us (75%)
  waiting for transfers between devices  8.47 us (8%)
  other arithmetic  7.38 us (7%)
  starting transfers between devices  3.62 us (4%)
  local copies, waits for them, and re-layouts  2.78 us (3%)
  between operations  2.73 us (3%)
    pallas_call x1, Pallas kernels, reduce_blocks(): pl.pallas_call(functools.partial(reduce_kernel, n_dp, n_col), out_shape=(...  54.4 us
    pallas_call x1, Pallas kernels, group_sum(): pl.pallas_call(functools.partial(norm_kernel, n_row, n_col), out_shape=ja...  22.8 us
    all_to_all x1, waiting for transfers between devices, shards(): lax.all_to_all(master_new, 'col', split_axis=1, concat_axis=0, tiled=True)  8.47 us
    all_to_all x1, starting transfers between devices, shards(): lax.all_to_all(master_new, 'col', split_axis=1, concat_axis=0, tiled=True)  3.62 us
    sub x1, other arithmetic, adam_step(): master_new = master - learn_rate * (direction + decay_weight * master)  2.73 us
  transfers between devices with their start and end apart: 1, of which 1 were waited for; matrix products, arithmetic and copies ran while one was open for 1% of the time, Pallas kernels for 0%

profile of v3, /device:TPU:1, one launch (start us, length us, event | category | flops | bytes accessed | tf_op | source)
XLA Modules:
  0.0 102.2 jit_solution(9670533789246923023)
XLA Ops:
  0.6 54.4 %shard_map.161 = (f32[128,1024]{1,0:T(8,128)}, f32[4,256]{1,0:T(4,128)}) custom-call(bf16[512,256]{1,0:T(8,128)(2,1)} %bitcast.12, bf16[4,256]{1,0:T(4,128)(2,1)} %bitcast.13), custom_call_target="tpu_custom_call" | custom-call | tf_op jit(solution)/shard_map/pallas_call | solution.py:252
  55.0 0.0 copy-start.1
  55.1 1.3 %multiply_reduce_fusion.1 = f32[]{:T(128)} fusion(f32[4,256]{1,0:T(4,128)} %get-tuple-element.11), kind=kLoop, calls=%fused_computation.13 | loop fusion | flops 2047 | bytes 4100 | tf_op jit(solution)/shard_map/reduce_sum | solution.py:45
  56.4 1.8 %multiply_reduce_fusion = f32[]{:T(128)} fusion(f32[128,1024]{1,0:T(8,128)} %get-tuple-element.10), kind=kLoop, calls=%fused_computation.6 | loop fusion | flops 262143 | bytes 524292 | tf_op jit(solution)/shard_map/reduce_sum | solution.py:45
  59.5 0.6 broadcast_in_dim.3.x_ref
  60.1 22.8 %shard_map.162 = f32[8,128]{1,0:T(8,128)} custom-call(f32[8,128]{1,0:T(8,128)} %broadcast_in_dim.3.x_ref), custom_call_target="tpu_custom_call" | custom-call | tf_op jit(solution)/shard_map/pallas_call | solution.py:92
  82.8 1.2 %slice.3 = f32[1,1]{1,0:T(1,128)} slice(f32[8,128]{1,0:T(8,128)} %shard_map.162), slice={[0:1], [0:1]} | slice | bytes 8 | tf_op jit(solution)/shard_map/slice | solution.py:104
  84.7 0.0 copy-done.1
  84.7 2.7 %multiply_subtract_fusion = (f32[128,1024]{1,0:T(8,128)S(1)}, f32[128,1024]{1,0:T(8,128)}, f32[128,1024]{1,0:T(8,128)}) fusion(f32[128,1024]{1,0:T(8,128)} %param.12, f32[128,1024]{1,0:T(8,128)S(1)} %copy-done.1, f32[]{:T(128)} %bitcast.2, f32[128,1024]{1,0:T(8,128)} %param.13, f32[128,1024]{1,0:T(8,128)} %param.14), kind=kLoop, calls=%fused_computation.4 | loop fusion | flops 2097152 | bytes 3670020 | tf_op jit(solution)/shard_map/sub | solution.py:36
  87.5 0.0 copy-start
  87.5 0.9 copy.22
  88.4 0.1 copy-done
  88.4 0.0 copy-start.3
  88.4 0.0 copy-start.4
  88.4 0.0 copy-start.5
  88.4 0.0 copy-start.6
  88.4 0.0 copy-start.7
  88.5 3.6 %all-to-all-start = ((f32[128,4,256]{2,0,1:T(8,128)}), f32[128,4,256]{2,0,1:T(8,128)S(1)}, u32[]{:S(2)}, u32[]{:S(2)}) async-start(f32[128,4,256]{2,0,1:T(8,128)} %bitcast.10), calls=%async_computation | async-start | bytes 1048576 | tf_op jit(solution)/shard_map/all_to_all | solution.py:300
  92.1 0.0 copy-done.3
  92.1 0.0 copy-done.4
  92.1 0.0 copy-done.5
  92.1 0.0 copy-done.6
  92.1 0.0 copy-done.7
  92.1 0.6 multiply_add_fusion.1
  92.8 0.0 copy-start.2
  92.8 8.5 %all-to-all-done = f32[128,4,256]{2,0,1:T(8,128)S(1)} async-done(((f32[128,4,256]{2,0,1:T(8,128)}), f32[128,4,256]{2,0,1:T(8,128)S(1)}, u32[]{:S(2)}, u32[]{:S(2)}) %all-to-all-start) | async-done | bytes 524320 | tf_op jit(solution)/shard_map/all_to_all | solution.py:300
  101.3 0.0 copy-done.2
  101.3 0.9 bitcast_add_fusion
  (1 shorter events, 0.0 us)
Async XLA Ops:
  55.0 29.7 %copy-start.1 = (f32[128,1024]{1,0:T(8,128)S(1)}, f32[128,1024]{1,0:T(8,128)}, u32[]{:S(2)}) copy-start(f32[128,1024]{1,0:T(8,128)} %get-tuple-element.10) | copy-start | bytes 1572868
  87.5 1.0 copy-start
  88.4 3.6 %copy-start.3 = (f32[4,256]{1,0:T(4,128)S(1)}, f32[4,256]{1,0:T(4,128)}, u32[]{:S(2)}) copy-start(f32[4,256]{1,0:T(4,128)} %get-tuple-element.11) | copy-start | bytes 12292
  88.4 3.7 %copy-start.4 = (f32[4,256]{1,0:T(4,128)S(1)}, f32[4,256]{1,0:T(4,128)}, u32[]{:S(2)}) copy-start(f32[4,256]{1,0:T(4,128)} %param.19) | copy-start | bytes 12292
  88.4 3.7 %copy-start.5 = (f32[4,256]{1,0:T(4,128)S(1)}, f32[4,256]{1,0:T(4,128)}, u32[]{:S(2)}) copy-start(f32[4,256]{1,0:T(4,128)} %param.16) | copy-start | bytes 12292
  88.4 3.7 %copy-start.6 = (f32[4,256]{1,0:T(4,128)S(1)}, f32[4,256]{1,0:T(4,128)}, u32[]{:S(2)}) copy-start(f32[4,256]{1,0:T(4,128)} %param.17) | copy-start | bytes 12292
  88.4 3.7 %copy-start.7 = (f32[4,256]{1,0:T(4,128)S(1)}, f32[4,256]{1,0:T(4,128)}, u32[]{:S(2)}) copy-start(f32[4,256]{1,0:T(4,128)} %param.18) | copy-start | bytes 12292
  88.5 12.8 %all-to-all-start = ((f32[128,4,256]{2,0,1:T(8,128)}), f32[128,4,256]{2,0,1:T(8,128)S(1)}, u32[]{:S(2)}, u32[]{:S(2)}) async-start(f32[128,4,256]{2,0,1:T(8,128)} %bitcast.10), calls=%async_computation | async-start | bytes 1048576 | tf_op jit(solution)/shard_map/all_to_all | solution.py:300
  92.8 8.5 %copy-start.2 = (f32[512,256]{1,0:T(8,128)S(1)}, f32[512,256]{1,0:T(8,128)}, u32[]{:S(2)}) copy-start(f32[512,256]{1,0:T(8,128)} %param.15) | copy-start | bytes 1572868

commit v4 on v2

--- a/solution.py
+++ b/solution.py
@@ -45,9 +45,14 @@
     return jnp.sum(gradient * gradient) + jnp.sum(ln_gradient * ln_gradient) / row_count
 
 
-def norm_kernel(n_row, n_col, x_ref, o_ref, buf, send_sem, recv_sem):
+def finish_kernel(n_row, n_col, g_ref, lg_ref, m_ref, f_ref, s_ref, a_ref,
+                  lm_ref, lf_ref, ls_ref, la_ref,
+                  a_out, m_out, f_out, s_out, lm_out, lf_out, ls_out, la_out,
+                  nbuf, mbuf, n_send, n_recv, m_send, m_recv):
     d = lax.axis_index("dp")
-    me = lax.axis_index("row") * n_col + lax.axis_index("col")
+    r = lax.axis_index("row")
+    c = lax.axis_index("col")
+    me = r * n_col + c
     n = n_row * n_col
     barrier = pltpu.get_barrier_semaphore()
     for j in range(1, n):
@@ -56,52 +61,95 @@
             barrier, inc=1, device_id=(d, peer // n_col, peer % n_col), device_id_type=MESH
         )
     pl.semaphore_wait(barrier, n - 1)
+    g = g_ref[...]
+    lg = lg_ref[...]
+    part = jnp.sum(g * g) + jnp.sum(lg * lg) / float(n_row)
+    nbuf[me] = jnp.full(nbuf.shape[1:], part, jnp.float32)
+
+    def n_copy(j, peer, slot):
+        return pltpu.make_async_remote_copy(
+            src_ref=nbuf.at[slot],
+            dst_ref=nbuf.at[slot],
+            send_sem=n_send.at[j],
+            recv_sem=n_recv.at[slot],
+            device_id=(d, peer // n_col, peer % n_col),
+            device_id_type=MESH,
+        )
+
     copies = []
     for j in range(1, n):
-        peer = lax.rem(me + j, n)
-        copy = pltpu.make_async_remote_copy(
-            src_ref=x_ref,
-            dst_ref=buf.at[me],
-            send_sem=send_sem.at[j],
-            recv_sem=recv_sem.at[me],
-            device_id=(d, peer // n_col, peer % n_col),
-            device_id_type=MESH,
-        )
+        copy = n_copy(j, lax.rem(me + j, n), me)
         copy.start()
         copies.append(copy)
-    buf[me] = x_ref[...]
     for j in range(1, n):
         sender = lax.rem(me + n - j, n)
-        pltpu.make_async_remote_copy(
-            src_ref=x_ref,
-            dst_ref=buf.at[sender],
-            send_sem=send_sem.at[j],
-            recv_sem=recv_sem.at[sender],
-            device_id=(d, sender // n_col, sender % n_col),
-            device_id_type=MESH,
-        ).wait_recv()
+        n_copy(j, sender, sender).wait_recv()
     for copy in copies:
         copy.wait_send()
-    o_ref[...] = jnp.sum(buf[...], axis=0)
-
-
-def group_sum(value):
+    norm_total = jnp.sum(nbuf[...], axis=0)[0:1, 0:1]
+    clip_scale = clip_factor(norm_total)
+    master_new, first_new, second_new = adam_step(
+        g, clip_scale, f_ref[...], s_ref[...], m_ref[...], decay_rate
+    )
+    m_out[...] = master_new
+    f_out[...] = first_new
+    s_out[...] = second_new
+    width = mbuf.shape[2]
+
+    def m_copy(j, peer, slot):
+        return pltpu.make_async_remote_copy(
+            src_ref=m_out.at[:, pl.ds(pl.multiple_of(peer * width, width), width)],
+            dst_ref=mbuf.at[slot],
+            send_sem=m_send.at[j],
+            recv_sem=m_recv.at[slot],
+            device_id=(d, r, peer),
+            device_id_type=MESH,
+        )
+
+    copies = []
+    for j in range(1, n_col):
+        copy = m_copy(j, lax.rem(c + j, n_col), c)
+        copy.start()
+        copies.append(copy)
+    mbuf[c] = m_out[:, pl.ds(pl.multiple_of(c * width, width), width)]
+    ln_master_new, ln_first_new, ln_second_new = adam_step(
+        lg, clip_scale, lf_ref[...], ls_ref[...], lm_ref[...], 0.0
+    )
+    lm_out[...] = ln_master_new
+    lf_out[...] = ln_first_new
+    ls_out[...] = ln_second_new
+    la_out[...] = ema_keep * la_ref[...] + (1.0 - ema_keep) * ln_master_new
+    for j in range(1, n_col):
+        sender = lax.rem(c + n_col - j, n_col)
+        m_copy(j, sender, sender).wait_recv()
+    for copy in copies:
+        copy.wait_send()
+    depth = mbuf.shape[1]
+    for q in range(n_col):
+        rows = pl.ds(q * depth, depth)
+        a_out[rows, :] = ema_keep * a_ref[rows, :] + (1.0 - ema_keep) * mbuf[q]
+
+
+def finish(gradient, ln_gradient, master, first, second, average, ln_master, ln_first, ln_second, ln_average):
     n_row, n_col = lax.axis_size("row"), lax.axis_size("col")
     n = n_row * n_col
-    tile = jnp.full((8, 128), value, jnp.float32)
-    out = pl.pallas_call(
-        functools.partial(norm_kernel, n_row, n_col),
-        out_shape=jax.ShapeDtypeStruct((8, 128), jnp.float32),
-        in_specs=[pl.BlockSpec(memory_space=pltpu.VMEM)],
-        out_specs=pl.BlockSpec(memory_space=pltpu.VMEM),
+    vmem = pl.BlockSpec(memory_space=pltpu.VMEM)
+    outs = (average, master, first, second, ln_master, ln_first, ln_second, ln_average)
+    return pl.pallas_call(
+        functools.partial(finish_kernel, n_row, n_col),
+        out_shape=tuple(jax.ShapeDtypeStruct(x.shape, jnp.float32) for x in outs),
+        in_specs=[vmem] * 10,
+        out_specs=tuple([vmem] * 8),
         scratch_shapes=[
             pltpu.VMEM((n, 8, 128), jnp.float32),
+            pltpu.VMEM((n_col, master.shape[0], average.shape[1]), jnp.float32),
             pltpu.SemaphoreType.DMA((n,)),
             pltpu.SemaphoreType.DMA((n,)),
+            pltpu.SemaphoreType.DMA((n_col,)),
+            pltpu.SemaphoreType.DMA((n_col,)),
         ],
         compiler_params=pltpu.CompilerParams(collective_id=0, has_side_effects=True),
-    )(tile)
-    return out[0, 0]
+    )(gradient, ln_gradient, master, first, second, average, ln_master, ln_first, ln_second, ln_average)
 
 
 def reduce_kernel(n_dp, n_col, g_ref, ln_ref, g_out, ln_out, rs_buf, ag_buf, ln_buf,
@@ -281,19 +329,20 @@
     ln_second,
     ln_average,
 ):
-    row_count = float(lax.axis_size("row"))
     gradient, ln_gradient = reduce_blocks(grad_blocks[0], ln_grads[0])
-    norm_total = group_sum(squares(gradient, ln_gradient, row_count))
-    clip_scale = clip_factor(norm_total)
-    master_new, first_new, second_new = adam_step(
-        gradient, clip_scale, first_moment, second_moment, master, decay_rate
-    )
-    ln_master_new, ln_first_new, ln_second_new = adam_step(
-        ln_gradient, clip_scale, ln_first, ln_second, ln_master, 0.0
-    )
-    ln_average_new = ema_keep * ln_average + (1.0 - ema_keep) * ln_master_new
-    block_master = lax.all_to_all(master_new, "col", split_axis=1, concat_axis=0, tiled=True)
-    average_new = ema_keep * average + (1.0 - ema_keep) * block_master
+    (
+        average_new,
+        master_new,
+        first_new,
+        second_new,
+        ln_master_new,
+        ln_first_new,
+        ln_second_new,
+        ln_average_new,
+    ) = finish(
+        gradient, ln_gradient, master, first_moment, second_moment, average,
+        ln_master, ln_first, ln_second, ln_average,
+    )
     return (
         average_new,
         master_new,

time: 97 us -> 91.7 us (0.945)
  Pallas kernels: 71.6 us -> 82.8 us
  waiting for transfers between devices: 8.47 us -> 0 us
  other arithmetic: 7.38 us -> 0 us
  local copies, waits for them, and re-layouts: 2.78 us -> 7.8 us
  starting transfers between devices: 3.62 us -> 0 us
  between operations: 2.73 us -> 0.67 us
    pallas_call x1, Pallas kernels: 14.2 us -> 25.5 us  [finish(): pl.pallas_call(functools.partial(finish_kernel, n_row, n_col), out_shape=...]
    all_to_all x1 -> x0, waiting for transfers between devices: 8.47 us -> none  [shards(): lax.all_to_all(master_new, 'col', split_axis=1, concat_axis=0, tiled=True)]
    unnamed x16 -> x22, local copies, waits for them, and re-layouts: 0.09 us -> 7.8 us
    all_to_all x1 -> x0, starting transfers between devices: 3.62 us -> none  [shards(): lax.all_to_all(master_new, 'col', split_axis=1, concat_axis=0, tiled=True)]
    reduce_sum x2 -> x0, other arithmetic: 3.11 us -> none  [the longest x1 1.78 us: squares(): jnp.sum(gradient * gradient)]
    sub x1 -> x0, other arithmetic: 2.73 us -> none  [adam_step(): master_new = master - learn_rate * (direction + decay_weight * master)]
    add x2 -> x0, other arithmetic: 1.49 us -> none  [the longest x1 0.86 us: shards(): average_new = ema_keep * average + (1.0 - ema_keep) * block_master]
    slice x1 -> x0, local copies, waits for them, and re-layouts: 1.19 us -> none  [group_sum(): return out[0, 0]]
  transfers between devices with their start and end apart: 1 -> 0, of which waited for: 1 -> 0; matrix products, arithmetic and copies ran while one was open for 1% -> 0% of each run, Pallas kernels for 0% -> 0%
where the time goes in v4:
time: 91.7 us; the launch traced here: 91.3 us
  Pallas kernels  82.8 us (90%)
  local copies, waits for them, and re-layouts  7.8 us (9%)
    pallas_call x1, Pallas kernels, reduce_blocks(): pl.pallas_call(functools.partial(reduce_kernel, n_dp, n_col), out_shape=(...  57.4 us
    pallas_call x1, Pallas kernels, finish(): pl.pallas_call(functools.partial(finish_kernel, n_row, n_col), out_shape=...  25.5 us
    unnamed x22, local copies, waits for them, and re-layouts  7.8 us

profile of v4, /device:TPU:1, one launch (start us, length us, event | category | flops | bytes accessed | tf_op | source)
XLA Modules:
  0.0 91.3 jit_solution(14652643268984576428)
XLA Ops:
  0.6 57.4 %shard_map.161 = (f32[128,1024]{1,0:T(8,128)}, f32[4,256]{1,0:T(4,128)}) custom-call(bf16[512,256]{1,0:T(8,128)(2,1)} %bitcast.2, bf16[4,256]{1,0:T(4,128)(2,1)} %bitcast.3), custom_call_target="tpu_custom_call" | custom-call | tf_op jit(solution)/shard_map/pallas_call | solution.py:297
  58.0 25.5 %shard_map.162 = (f32[512,256]{1,0:T(8,128)}, f32[128,1024]{1,0:T(8,128)}, f32[128,1024]{1,0:T(8,128)}, f32[128,1024]{1,0:T(8,128)}, f32[4,256]{1,0:T(4,128)}, /...) custom-call(f32[128,1024]{1,0:T(8,128)} %get-tuple-element.10.g_ref, f32[4,256]{1,0:T(4,128)} %get-tuple-element.11.lg_ref, ...), custom_call_target="tpu_custom_call" | custom-call | tf_op jit(solution)/shard_map/pallas_call | solution.py:138
  83.5 0.0 copy-start.2
  83.5 1.9 %copy.26 = f32[512,256]{1,0:T(8,128)} copy(f32[512,256]{1,0:T(8,128)} %get-tuple-element.20) | data formatting | bytes 1048576
  85.4 0.0 copy-done.2
  85.4 0.0 copy-start.1
  85.4 0.8 copy.27
  86.2 0.4 copy-done.1
  86.7 0.0 copy-start
  86.7 0.8 copy.28
  87.5 0.4 copy-done
  87.9 0.0 copy-start.6
  87.9 0.8 copy.29
  88.7 0.0 copy-done.6
  88.7 0.0 copy-start.5
  88.7 0.6 copy.30
  89.3 0.1 copy-done.5
  89.4 0.0 copy-start.4
  89.4 0.6 copy.31
  90.0 0.1 copy-done.4
  90.0 0.0 copy-start.3
  90.1 0.6 copy.32
  90.6 0.1 copy-done.3
  90.7 0.6 copy.33
Async XLA Ops:
  83.5 1.9 %copy-start.2 = (f32[128,1024]{1,0:T(8,128)S(1)}, f32[128,1024]{1,0:T(8,128)}, u32[]{:S(2)}) copy-start(f32[128,1024]{1,0:T(8,128)} %get-tuple-element.21) | copy-start | bytes 1572868
  85.4 1.2 %copy-start.1 = (f32[128,1024]{1,0:T(8,128)S(1)}, f32[128,1024]{1,0:T(8,128)}, u32[]{:S(2)}) copy-start(f32[128,1024]{1,0:T(8,128)} %get-tuple-element.22) | copy-start | bytes 1572868
  86.7 1.2 %copy-start = (f32[128,1024]{1,0:T(8,128)S(1)}, f32[128,1024]{1,0:T(8,128)}, u32[]{:S(2)}) copy-start(f32[128,1024]{1,0:T(8,128)} %get-tuple-element.23) | copy-start | bytes 1572868
  87.9 0.8 copy-start.6
  88.7 0.7 copy-start.5
  89.4 0.7 copy-start.4
  90.0 0.7 copy-start.3

commit v5 on v4

--- a/solution.py
+++ b/solution.py
@@ -45,10 +45,8 @@
     return jnp.sum(gradient * gradient) + jnp.sum(ln_gradient * ln_gradient) / row_count
 
 
-def finish_kernel(n_row, n_col, g_ref, lg_ref, m_ref, f_ref, s_ref, a_ref,
-                  lm_ref, lf_ref, ls_ref, la_ref,
-                  a_out, m_out, f_out, s_out, lm_out, lf_out, ls_out, la_out,
-                  nbuf, mbuf, n_send, n_recv, m_send, m_recv):
+def finish_kernel(n_row, n_col, g_ref, lg_ref, m_ref, f_ref, s_ref, c_out, b_out,
+                  nbuf, mbuf, rbuf, n_send, n_recv, m_send, m_recv):
     d = lax.axis_index("dp")
     r = lax.axis_index("row")
     c = lax.axis_index("col")
@@ -88,18 +86,15 @@
         copy.wait_send()
     norm_total = jnp.sum(nbuf[...], axis=0)[0:1, 0:1]
     clip_scale = clip_factor(norm_total)
-    master_new, first_new, second_new = adam_step(
-        g, clip_scale, f_ref[...], s_ref[...], m_ref[...], decay_rate
-    )
-    m_out[...] = master_new
-    f_out[...] = first_new
-    s_out[...] = second_new
-    width = mbuf.shape[2]
+    c_out[...] = jnp.broadcast_to(clip_scale, c_out.shape)
+    master_new, _, _ = adam_step(g, clip_scale, f_ref[...], s_ref[...], m_ref[...], decay_rate)
+    mbuf[c] = master_new
+    width = b_out.shape[1]
 
     def m_copy(j, peer, slot):
         return pltpu.make_async_remote_copy(
-            src_ref=m_out.at[:, pl.ds(pl.multiple_of(peer * width, width), width)],
-            dst_ref=mbuf.at[slot],
+            src_ref=mbuf.at[c, :, pl.ds(pl.multiple_of(peer * width, width), width)],
+            dst_ref=rbuf.at[slot],
             send_sem=m_send.at[j],
             recv_sem=m_recv.at[slot],
             device_id=(d, r, peer),
@@ -111,45 +106,41 @@
         copy = m_copy(j, lax.rem(c + j, n_col), c)
         copy.start()
         copies.append(copy)
-    mbuf[c] = m_out[:, pl.ds(pl.multiple_of(c * width, width), width)]
-    ln_master_new, ln_first_new, ln_second_new = adam_step(
-        lg, clip_scale, lf_ref[...], ls_ref[...], lm_ref[...], 0.0
-    )
-    lm_out[...] = ln_master_new
-    lf_out[...] = ln_first_new
-    ls_out[...] = ln_second_new
-    la_out[...] = ema_keep * la_ref[...] + (1.0 - ema_keep) * ln_master_new
+    rbuf[c] = mbuf[c, :, pl.ds(pl.multiple_of(c * width, width), width)]
     for j in range(1, n_col):
         sender = lax.rem(c + n_col - j, n_col)
         m_copy(j, sender, sender).wait_recv()
     for copy in copies:
         copy.wait_send()
-    depth = mbuf.shape[1]
+    depth = rbuf.shape[1]
     for q in range(n_col):
-        rows = pl.ds(q * depth, depth)
-        a_out[rows, :] = ema_keep * a_ref[rows, :] + (1.0 - ema_keep) * mbuf[q]
-
-
-def finish(gradient, ln_gradient, master, first, second, average, ln_master, ln_first, ln_second, ln_average):
+        b_out[pl.ds(q * depth, depth), :] = rbuf[q]
+
+
+def finish(gradient, ln_gradient, master, first, second, average):
     n_row, n_col = lax.axis_size("row"), lax.axis_size("col")
     n = n_row * n_col
     vmem = pl.BlockSpec(memory_space=pltpu.VMEM)
-    outs = (average, master, first, second, ln_master, ln_first, ln_second, ln_average)
+    rows, width = master.shape[0], average.shape[1]
     return pl.pallas_call(
         functools.partial(finish_kernel, n_row, n_col),
-        out_shape=tuple(jax.ShapeDtypeStruct(x.shape, jnp.float32) for x in outs),
-        in_specs=[vmem] * 10,
-        out_specs=tuple([vmem] * 8),
+        out_shape=(
+            jax.ShapeDtypeStruct((8, 128), jnp.float32),
+            jax.ShapeDtypeStruct(average.shape, jnp.float32),
+        ),
+        in_specs=[vmem] * 5,
+        out_specs=(vmem, vmem),
         scratch_shapes=[
             pltpu.VMEM((n, 8, 128), jnp.float32),
-            pltpu.VMEM((n_col, master.shape[0], average.shape[1]), jnp.float32),
+            pltpu.VMEM((n_col,) + master.shape, jnp.float32),
+            pltpu.VMEM((n_col, rows, width), jnp.float32),
             pltpu.SemaphoreType.DMA((n,)),
             pltpu.SemaphoreType.DMA((n,)),
             pltpu.SemaphoreType.DMA((n_col,)),
             pltpu.SemaphoreType.DMA((n_col,)),
         ],
         compiler_params=pltpu.CompilerParams(collective_id=0, has_side_effects=True),
-    )(gradient, ln_gradient, master, first, second, average, ln_master, ln_first, ln_second, ln_average)
+    )(gradient, ln_gradient, master, first, second)
 
 
 def reduce_kernel(n_dp, n_col, g_ref, ln_ref, g_out, ln_out, rs_buf, ag_buf, ln_buf,
@@ -330,19 +321,18 @@
     ln_average,
 ):
     gradient, ln_gradient = reduce_blocks(grad_blocks[0], ln_grads[0])
-    (
-        average_new,
-        master_new,
-        first_new,
-        second_new,
-        ln_master_new,
-        ln_first_new,
-        ln_second_new,
-        ln_average_new,
-    ) = finish(
-        gradient, ln_gradient, master, first_moment, second_moment, average,
-        ln_master, ln_first, ln_second, ln_average,
-    )
+    clip_tile, block_master = finish(
+        gradient, ln_gradient, master, first_moment, second_moment, average
+    )
+    clip_scale = clip_tile[0, 0]
+    master_new, first_new, second_new = adam_step(
+        gradient, clip_scale, first_moment, second_moment, master, decay_rate
+    )
+    ln_master_new, ln_first_new, ln_second_new = adam_step(
+        ln_gradient, clip_scale, ln_first, ln_second, ln_master, 0.0
+    )
+    ln_average_new = ema_keep * ln_average + (1.0 - ema_keep) * ln_master_new
+    average_new = ema_keep * average + (1.0 - ema_keep) * block_master
     return (
         average_new,
         master_new,

time: 91.7 us -> 90.5 us (0.987)
  local copies, waits for them, and re-layouts: 7.8 us -> 1.96 us
  other arithmetic: 0 us -> 5.45 us
    unnamed x22 -> x20, local copies, waits for them, and re-layouts: 7.8 us -> 0.71 us
    add x0 -> x2, other arithmetic: none -> 3.33 us  [the longest x1 2.03 us: shards(): average_new = ema_keep * average + (1.0 - ema_keep) * block_master]
    sub x0 -> x1, other arithmetic: none -> 2.12 us  [adam_step(): master_new = master - learn_rate * (direction + decay_weight * master)]
    slice x0 -> x1, local copies, waits for them, and re-layouts: none -> 1.26 us  [shards(): clip_scale = clip_tile[0, 0]]
where the time goes in v5:
time: 90.5 us; the launch traced here: 90.2 us
  Pallas kernels  82 us (91%)
  other arithmetic  5.45 us (6%)
  local copies, waits for them, and re-layouts  1.96 us (2%)
    pallas_call x1, Pallas kernels, reduce_blocks(): pl.pallas_call(functools.partial(reduce_kernel, n_dp, n_col), out_shape=(...  57.4 us
    pallas_call x1, Pallas kernels, finish(): pl.pallas_call(functools.partial(finish_kernel, n_row, n_col), out_shape=...  24.7 us
    sub x1, other arithmetic, adam_step(): master_new = master - learn_rate * (direction + decay_weight * master)  2.12 us
    add x1, other arithmetic, shards(): average_new = ema_keep * average + (1.0 - ema_keep) * block_master  2.03 us

profile of v5, /device:TPU:1, one launch (start us, length us, event | category | flops | bytes accessed | tf_op | source)
XLA Modules:
  0.0 90.2 jit_solution(15586553619967781947)
XLA Ops:
  0.6 57.4 %shard_map.161 = (f32[128,1024]{1,0:T(8,128)}, f32[4,256]{1,0:T(4,128)}) custom-call(bf16[512,256]{1,0:T(8,128)(2,1)} %bitcast.3, bf16[4,256]{1,0:T(4,128)(2,1)} %bitcast.4), custom_call_target="tpu_custom_call" | custom-call | tf_op jit(solution)/shard_map/pallas_call | solution.py:288
  58.0 0.0 copy-start.4
  58.0 0.0 copy-start.3
  58.0 24.7 %shard_map.162 = (f32[8,128]{1,0:T(8,128)}, f32[512,256]{1,0:T(8,128)}) custom-call(f32[128,1024]{1,0:T(8,128)} %get-tuple-element.12.g_ref, f32[4,256]{1,0:T(4,128)} %get-tuple-element.13.lg_ref, f32[128,1024]{1,0:T(8,128)} %m_ref.1, f32[128,1024]{1,0:T(8,128)} %f_ref.1, f32[128,1024]{1,0:T(8,128)} %s_ref.1), custom_call_target="tpu_custom_call" | custom-call | tf_op jit(solution)/shard_map/pallas_call | solution.py:125
  82.7 0.0 copy-done.4
  82.7 0.0 copy-start
  82.7 0.0 copy-start.1
  82.7 0.0 copy-start.2
  82.7 2.0 %multiply_add_fusion.1 = f32[512,256]{1,0:T(8,128)} fusion(f32[512,256]{1,0:T(8,128)} %get-tuple-element.14, f32[512,256]{1,0:T(8,128)S(1)} %copy-done.4), kind=kLoop, calls=%fused_computation.4 | loop fusion | flops 393216 | bytes 1572864 | tf_op jit(solution)/shard_map/add | solution.py:335
  84.8 1.3 %slice.3 = f32[1,1]{1,0:T(1,128)} slice(f32[8,128]{1,0:T(8,128)} %get-tuple-element.15), slice={[0:1], [0:1]} | slice | bytes 8 | tf_op jit(solution)/shard_map/slice | solution.py:327
  86.0 0.0 copy-done.3
  86.0 0.0 copy-done
  86.0 0.0 copy-done.1
  86.0 0.0 copy-done.2
  86.0 0.0 copy-start.6
  86.0 0.0 copy-start.7
  86.1 0.0 copy-start.8
  86.1 0.0 copy-start.9
  86.1 2.1 %multiply_subtract_fusion = (f32[128,1024]{1,0:T(8,128)}, f32[128,1024]{1,0:T(8,128)}, f32[128,1024]{1,0:T(8,128)}) fusion(f32[128,1024]{1,0:T(8,128)S(1)} %copy-done, f32[128,1024]{1,0:T(8,128)S(1)} %copy-done.3, f32[]{:T(128)} %bitcast.2, f32[128,1024]{1,0:T(8,128)S(1)} %copy-done.1, f32[128,1024]{1,0:T(8,128)S(1)} %copy-done.2), kind=kLoop, calls=%fused_computation.2 | loop fusion | flops 2097152 | bytes 3670020 | tf_op jit(solution)/shard_map/sub | solution.py:36
  88.2 0.0 copy-start.5
  88.2 0.0 copy-done.6
  88.2 0.0 copy-done.7
  88.2 0.0 copy-done.8
  88.2 0.0 copy-done.9
  88.2 0.7 copy-done.5
  88.9 1.3 %multiply_add_fusion.2 = (f32[4,256]{1,0:T(4,128)}, f32[4,256]{1,0:T(4,128)}, f32[4,256]{1,0:T(4,128)}, f32[4,256]{1,0:T(4,128)}) fusion(f32[4,256]{1,0:T(4,128)S(1)} %copy-done.6, f32[4,256]{1,0:T(4,128)S(1)} %copy-done.7, f32[4,256]{1,0:T(4,128)S(1)} %copy-done.5, f32[]{:T(128)} %bitcast.2, f32[4,256]{1,0:T(4,128)S(1)} %copy-done.8, f32[4,256]{1,0:T(4,128)S(1)} %copy-done.9), kind=kLoop, calls=%fused_computation.7 | loop fusion | flops 19456 | bytes 36868 | tf_op jit(solution)/shard_map/add | solution.py:334
Async XLA Ops:
  58.0 24.7 %copy-start.4 = (f32[512,256]{1,0:T(8,128)S(1)}, f32[512,256]{1,0:T(8,128)}, u32[]{:S(2)}) copy-start(f32[512,256]{1,0:T(8,128)} %param.15) | copy-start | bytes 1572868
  58.0 28.0 %copy-start.3 = (f32[128,1024]{1,0:T(8,128)S(1)}, f32[128,1024]{1,0:T(8,128)}, u32[]{:S(2)}) copy-start(f32[128,1024]{1,0:T(8,128)} %get-tuple-element.12.g_ref) | copy-start | bytes 1572868
  82.7 3.3 %copy-start = (f32[128,1024]{1,0:T(8,128)S(1)}, f32[128,1024]{1,0:T(8,128)}, u32[]{:S(2)}) copy-start(f32[128,1024]{1,0:T(8,128)} %m_ref.1) | copy-start | bytes 1572868
  82.7 3.3 %copy-start.1 = (f32[128,1024]{1,0:T(8,128)S(1)}, f32[128,1024]{1,0:T(8,128)}, u32[]{:S(2)}) copy-start(f32[128,1024]{1,0:T(8,128)} %f_ref.1) | copy-start | bytes 1572868
  82.7 3.3 %copy-start.2 = (f32[128,1024]{1,0:T(8,128)S(1)}, f32[128,1024]{1,0:T(8,128)}, u32[]{:S(2)}) copy-start(f32[128,1024]{1,0:T(8,128)} %s_ref.1) | copy-start | bytes 1572868
  86.0 2.2 %copy-start.6 = (f32[4,256]{1,0:T(4,128)S(1)}, f32[4,256]{1,0:T(4,128)}, u32[]{:S(2)}) copy-start(f32[4,256]{1,0:T(4,128)} %param.19) | copy-start | bytes 12292
  86.0 2.2 %copy-start.7 = (f32[4,256]{1,0:T(4,128)S(1)}, f32[4,256]{1,0:T(4,128)}, u32[]{:S(2)}) copy-start(f32[4,256]{1,0:T(4,128)} %param.16) | copy-start | bytes 12292
  86.1 2.2 %copy-start.8 = (f32[4,256]{1,0:T(4,128)S(1)}, f32[4,256]{1,0:T(4,128)}, u32[]{:S(2)}) copy-start(f32[4,256]{1,0:T(4,128)} %param.17) | copy-start | bytes 12292
  86.1 2.1 %copy-start.9 = (f32[4,256]{1,0:T(4,128)S(1)}, f32[4,256]{1,0:T(4,128)}, u32[]{:S(2)}) copy-start(f32[4,256]{1,0:T(4,128)} %param.18) | copy-start | bytes 12292
  88.2 0.7 copy-start.5

commit v6 on v5

--- a/solution.py
+++ b/solution.py
@@ -222,22 +222,38 @@
     lax.fori_loop(1, n, wait_rs, 0)
     ag_buf[d] = jnp.sum(rs_buf[...].astype(jnp.float32), axis=0)
 
-    def ag_copy(j):
-        peer = lax.rem(d + j, n_dp)
-        return pltpu.make_async_remote_copy(
-            src_ref=ag_buf.at[d],
-            dst_ref=ag_buf.at[d],
+    def ag_copy(slot, j, peer):
+        return pltpu.make_async_remote_copy(
+            src_ref=ag_buf.at[slot],
+            dst_ref=ag_buf.at[slot],
             send_sem=ag_send.at[j],
-            recv_sem=ag_recv.at[d],
+            recv_sem=ag_recv.at[slot],
             device_id=(peer, r, c),
             device_id_type=MESH,
         )
 
-    def start_ag(j, carry):
-        ag_copy(j).start()
-        return carry
-
-    lax.fori_loop(1, n_dp, start_ag, 0)
+    def arrive(slot):
+        ag_copy(slot, 0, slot).wait_recv()
+
+    reach = 3
+    n_right = n_dp // 2
+    n_left = n_dp - 1 - n_right
+    sends = []
+    waited = set()
+    for leg in range(0, n_right, reach):
+        for sign, span in ((1, n_right), (-1, n_left)):
+            if leg >= span:
+                continue
+            back = (n_dp - sign * leg) % n_dp
+            slot = lax.rem(d + back, n_dp)
+            if leg:
+                arrive(slot)
+                waited.add(back)
+            for hop in range(1, min(reach, span - leg) + 1):
+                peer = lax.rem(d + (n_dp + sign * hop) % n_dp, n_dp)
+                copy = ag_copy(slot, len(sends), peer)
+                copy.start()
+                sends.append(copy)
 
     def wait_ln(j, carry):
         src = lax.rem(d + j, n_dp)
@@ -255,20 +271,11 @@
     lax.fori_loop(1, n_dp, wait_ln, 0)
     ln_out[...] = jnp.sum(ln_buf[...].astype(jnp.float32), axis=0)
 
-    def wait_ag(j, carry):
-        src = lax.rem(d + j, n_dp)
-        pltpu.make_async_remote_copy(
-            src_ref=ag_buf.at[src],
-            dst_ref=ag_buf.at[src],
-            send_sem=ag_send.at[j],
-            recv_sem=ag_recv.at[src],
-            device_id=(src, r, c),
-            device_id_type=MESH,
-        ).wait_recv()
-        ag_copy(j).wait_send()
-        return carry
-
-    lax.fori_loop(1, n_dp, wait_ag, 0)
+    for back in range(1, n_dp):
+        if back not in waited:
+            arrive(lax.rem(d + back, n_dp))
+    for copy in sends:
+        copy.wait_send()
     for k in range(n_dp):
         for q in range(n_col):
             g_out[

time: 90.5 us -> 88.7 us (0.980)
  Pallas kernels: 82 us -> 80.2 us
    pallas_call x1, Pallas kernels: 57.4 us -> 49.5 us  [reduce_blocks(): pl.pallas_call(functools.partial(reduce_kernel, n_dp, n_col), out_shape=(...]
    pallas_call x1, Pallas kernels: 24.7 us -> 30.7 us  [finish(): pl.pallas_call(functools.partial(finish_kernel, n_row, n_col), out_shape=...]
where the time goes in v6:
time: 88.7 us; the launch traced here: 88.4 us
  Pallas kernels  80.2 us (90%)
  other arithmetic  5.45 us (6%)
  local copies, waits for them, and re-layouts  1.96 us (2%)
    pallas_call x1, Pallas kernels, reduce_blocks(): pl.pallas_call(functools.partial(reduce_kernel, n_dp, n_col), out_shape=(...  49.5 us
    pallas_call x1, Pallas kernels, finish(): pl.pallas_call(functools.partial(finish_kernel, n_row, n_col), out_shape=...  30.7 us
    sub x1, other arithmetic, adam_step(): master_new = master - learn_rate * (direction + decay_weight * master)  2.12 us
    add x1, other arithmetic, shards(): average_new = ema_keep * average + (1.0 - ema_keep) * block_master  2.03 us

profile of v6, /device:TPU:1, one launch (start us, length us, event | category | flops | bytes accessed | tf_op | source)
XLA Modules:
  0.0 88.4 jit_solution(16315455842940876035)
XLA Ops:
  0.6 49.5 %shard_map.161 = (f32[128,1024]{1,0:T(8,128)}, f32[4,256]{1,0:T(4,128)}) custom-call(bf16[512,256]{1,0:T(8,128)(2,1)} %bitcast.3, bf16[4,256]{1,0:T(4,128)(2,1)} %bitcast.4), custom_call_target="tpu_custom_call" | custom-call | tf_op jit(solution)/shard_map/pallas_call | solution.py:295
  50.2 0.0 copy-start.4
  50.2 0.0 copy-start.3
  50.2 30.7 %shard_map.162 = (f32[8,128]{1,0:T(8,128)}, f32[512,256]{1,0:T(8,128)}) custom-call(f32[128,1024]{1,0:T(8,128)} %get-tuple-element.12.g_ref, f32[4,256]{1,0:T(4,128)} %get-tuple-element.13.lg_ref, f32[128,1024]{1,0:T(8,128)} %m_ref.1, f32[128,1024]{1,0:T(8,128)} %f_ref.1, f32[128,1024]{1,0:T(8,128)} %s_ref.1), custom_call_target="tpu_custom_call" | custom-call | tf_op jit(solution)/shard_map/pallas_call | solution.py:125
  80.9 0.0 copy-done.4
  80.9 0.0 copy-start
  80.9 0.0 copy-start.1
  80.9 0.0 copy-start.2
  80.9 2.0 %multiply_add_fusion.1 = f32[512,256]{1,0:T(8,128)} fusion(f32[512,256]{1,0:T(8,128)} %get-tuple-element.14, f32[512,256]{1,0:T(8,128)S(1)} %copy-done.4), kind=kLoop, calls=%fused_computation.4 | loop fusion | flops 393216 | bytes 1572864 | tf_op jit(solution)/shard_map/add | solution.py:342
  83.0 1.3 %slice.3 = f32[1,1]{1,0:T(1,128)} slice(f32[8,128]{1,0:T(8,128)} %get-tuple-element.15), slice={[0:1], [0:1]} | slice | bytes 8 | tf_op jit(solution)/shard_map/slice | solution.py:334
  84.2 0.0 copy-done.3
  84.2 0.0 copy-done
  84.2 0.0 copy-done.1
  84.2 0.0 copy-done.2
  84.3 0.0 copy-start.6
  84.3 0.0 copy-start.7
  84.3 0.0 copy-start.8
  84.3 0.0 copy-start.9
  84.3 2.1 %multiply_subtract_fusion = (f32[128,1024]{1,0:T(8,128)}, f32[128,1024]{1,0:T(8,128)}, f32[128,1024]{1,0:T(8,128)}) fusion(f32[128,1024]{1,0:T(8,128)S(1)} %copy-done, f32[128,1024]{1,0:T(8,128)S(1)} %copy-done.3, f32[]{:T(128)} %bitcast.2, f32[128,1024]{1,0:T(8,128)S(1)} %copy-done.1, f32[128,1024]{1,0:T(8,128)S(1)} %copy-done.2), kind=kLoop, calls=%fused_computation.2 | loop fusion | flops 2097152 | bytes 3670020 | tf_op jit(solution)/shard_map/sub | solution.py:36
  86.4 0.0 copy-start.5
  86.4 0.0 copy-done.6
  86.4 0.0 copy-done.7
  86.4 0.0 copy-done.8
  86.4 0.0 copy-done.9
  86.4 0.7 copy-done.5
  87.1 1.3 %multiply_add_fusion.2 = (f32[4,256]{1,0:T(4,128)}, f32[4,256]{1,0:T(4,128)}, f32[4,256]{1,0:T(4,128)}, f32[4,256]{1,0:T(4,128)}) fusion(f32[4,256]{1,0:T(4,128)S(1)} %copy-done.6, f32[4,256]{1,0:T(4,128)S(1)} %copy-done.7, f32[4,256]{1,0:T(4,128)S(1)} %copy-done.5, f32[]{:T(128)} %bitcast.2, f32[4,256]{1,0:T(4,128)S(1)} %copy-done.8, f32[4,256]{1,0:T(4,128)S(1)} %copy-done.9), kind=kLoop, calls=%fused_computation.7 | loop fusion | flops 19456 | bytes 36868 | tf_op jit(solution)/shard_map/add | solution.py:341
Async XLA Ops:
  50.2 30.7 %copy-start.4 = (f32[512,256]{1,0:T(8,128)S(1)}, f32[512,256]{1,0:T(8,128)}, u32[]{:S(2)}) copy-start(f32[512,256]{1,0:T(8,128)} %param.15) | copy-start | bytes 1572868
  50.2 34.1 %copy-start.3 = (f32[128,1024]{1,0:T(8,128)S(1)}, f32[128,1024]{1,0:T(8,128)}, u32[]{:S(2)}) copy-start(f32[128,1024]{1,0:T(8,128)} %get-tuple-element.12.g_ref) | copy-start | bytes 1572868
  80.9 3.3 %copy-start = (f32[128,1024]{1,0:T(8,128)S(1)}, f32[128,1024]{1,0:T(8,128)}, u32[]{:S(2)}) copy-start(f32[128,1024]{1,0:T(8,128)} %m_ref.1) | copy-start | bytes 1572868
  80.9 3.3 %copy-start.1 = (f32[128,1024]{1,0:T(8,128)S(1)}, f32[128,1024]{1,0:T(8,128)}, u32[]{:S(2)}) copy-start(f32[128,1024]{1,0:T(8,128)} %f_ref.1) | copy-start | bytes 1572868
  80.9 3.3 %copy-start.2 = (f32[128,1024]{1,0:T(8,128)S(1)}, f32[128,1024]{1,0:T(8,128)}, u32[]{:S(2)}) copy-start(f32[128,1024]{1,0:T(8,128)} %s_ref.1) | copy-start | bytes 1572868
  84.3 2.2 %copy-start.6 = (f32[4,256]{1,0:T(4,128)S(1)}, f32[4,256]{1,0:T(4,128)}, u32[]{:S(2)}) copy-start(f32[4,256]{1,0:T(4,128)} %param.19) | copy-start | bytes 12292
  84.3 2.2 %copy-start.7 = (f32[4,256]{1,0:T(4,128)S(1)}, f32[4,256]{1,0:T(4,128)}, u32[]{:S(2)}) copy-start(f32[4,256]{1,0:T(4,128)} %param.16) | copy-start | bytes 12292
  84.3 2.2 %copy-start.8 = (f32[4,256]{1,0:T(4,128)S(1)}, f32[4,256]{1,0:T(4,128)}, u32[]{:S(2)}) copy-start(f32[4,256]{1,0:T(4,128)} %param.17) | copy-start | bytes 12292
  84.3 2.1 %copy-start.9 = (f32[4,256]{1,0:T(4,128)S(1)}, f32[4,256]{1,0:T(4,128)}, u32[]{:S(2)}) copy-start(f32[4,256]{1,0:T(4,128)} %param.18) | copy-start | bytes 12292
  86.4 0.7 copy-start.5

commit v7 on v6

--- a/solution.py
+++ b/solution.py
@@ -45,20 +45,13 @@
     return jnp.sum(gradient * gradient) + jnp.sum(ln_gradient * ln_gradient) / row_count
 
 
-def finish_kernel(n_row, n_col, g_ref, lg_ref, m_ref, f_ref, s_ref, c_out, b_out,
-                  nbuf, mbuf, rbuf, n_send, n_recv, m_send, m_recv):
+def finish_part(n_row, n_col, g_ref, lg_ref, m_ref, f_ref, s_ref, c_out, b_out,
+                nbuf, mbuf, rbuf, n_send, n_recv, m_send, m_recv):
     d = lax.axis_index("dp")
     r = lax.axis_index("row")
     c = lax.axis_index("col")
     me = r * n_col + c
     n = n_row * n_col
-    barrier = pltpu.get_barrier_semaphore()
-    for j in range(1, n):
-        peer = lax.rem(me + j, n)
-        pl.semaphore_signal(
-            barrier, inc=1, device_id=(d, peer // n_col, peer % n_col), device_id_type=MESH
-        )
-    pl.semaphore_wait(barrier, n - 1)
     g = g_ref[...]
     lg = lg_ref[...]
     part = jnp.sum(g * g) + jnp.sum(lg * lg) / float(n_row)
@@ -117,34 +110,10 @@
         b_out[pl.ds(q * depth, depth), :] = rbuf[q]
 
 
-def finish(gradient, ln_gradient, master, first, second, average):
-    n_row, n_col = lax.axis_size("row"), lax.axis_size("col")
-    n = n_row * n_col
-    vmem = pl.BlockSpec(memory_space=pltpu.VMEM)
-    rows, width = master.shape[0], average.shape[1]
-    return pl.pallas_call(
-        functools.partial(finish_kernel, n_row, n_col),
-        out_shape=(
-            jax.ShapeDtypeStruct((8, 128), jnp.float32),
-            jax.ShapeDtypeStruct(average.shape, jnp.float32),
-        ),
-        in_specs=[vmem] * 5,
-        out_specs=(vmem, vmem),
-        scratch_shapes=[
-            pltpu.VMEM((n, 8, 128), jnp.float32),
-            pltpu.VMEM((n_col,) + master.shape, jnp.float32),
-            pltpu.VMEM((n_col, rows, width), jnp.float32),
-            pltpu.SemaphoreType.DMA((n,)),
-            pltpu.SemaphoreType.DMA((n,)),
-            pltpu.SemaphoreType.DMA((n_col,)),
-            pltpu.SemaphoreType.DMA((n_col,)),
-        ],
-        compiler_params=pltpu.CompilerParams(collective_id=0, has_side_effects=True),
-    )(gradient, ln_gradient, master, first, second)
-
-
-def reduce_kernel(n_dp, n_col, g_ref, ln_ref, g_out, ln_out, rs_buf, ag_buf, ln_buf,
-                  rs_send, rs_recv, ag_send, ag_recv, ln_send, ln_recv):
+def reduce_kernel(n_dp, n_row, n_col, g_ref, ln_ref, m_ref, f_ref, s_ref,
+                  g_out, ln_out, c_out, b_out, rs_buf, ag_buf, ln_buf,
+                  rs_send, rs_recv, ag_send, ag_recv, ln_send, ln_recv,
+                  nbuf, mbuf, rbuf, n_send, n_recv, m_send, m_recv):
     d = lax.axis_index("dp")
     r = lax.axis_index("row")
     c = lax.axis_index("col")
@@ -164,7 +133,16 @@
         return carry
 
     lax.fori_loop(1, n, greet, 0)
-    pl.semaphore_wait(barrier, n - 1)
+
+    def greet_row(j, carry):
+        peer = lax.rem(r + 1 + j // n_col, n_row)
+        pl.semaphore_signal(
+            barrier, inc=1, device_id=(d, peer, j % n_col), device_id_type=MESH
+        )
+        return carry
+
+    lax.fori_loop(0, (n_row - 1) * n_col, greet_row, 0)
+    pl.semaphore_wait(barrier, n - 1 + (n_row - 1) * n_col)
 
     def piece(k, q):
         rows = pl.ds(pl.multiple_of(q * quarter + (k // halves) * depth, depth), depth)
@@ -282,24 +260,29 @@
                 pl.ds((k // halves) * depth, depth),
                 pl.ds(q * halves * width + (k % halves) * width, width),
             ] = ag_buf[k, q]
-
-
-def reduce_blocks(block, ln_part):
-    n_dp, n_col = lax.axis_size("dp"), lax.axis_size("col")
+    finish_part(n_row, n_col, g_out, ln_out, m_ref, f_ref, s_ref, c_out, b_out,
+                nbuf, mbuf, rbuf, n_send, n_recv, m_send, m_recv)
+
+
+def reduce_blocks(block, ln_part, master, first, second, average):
+    n_dp, n_row, n_col = lax.axis_size("dp"), lax.axis_size("row"), lax.axis_size("col")
     rows, cols = block.shape
     quarter = rows // n_col
     width = 128
     halves = cols // width
     depth = quarter * halves // n_dp
+    n = n_row * n_col
     vmem = pl.BlockSpec(memory_space=pltpu.VMEM)
     return pl.pallas_call(
-        functools.partial(reduce_kernel, n_dp, n_col),
+        functools.partial(reduce_kernel, n_dp, n_row, n_col),
         out_shape=(
             jax.ShapeDtypeStruct((quarter, cols * n_col), jnp.float32),
             jax.ShapeDtypeStruct(ln_part.shape, jnp.float32),
+            jax.ShapeDtypeStruct((8, 128), jnp.float32),
+            jax.ShapeDtypeStruct(average.shape, jnp.float32),
         ),
-        in_specs=[vmem, vmem],
-        out_specs=(vmem, vmem),
+        in_specs=[vmem] * 5,
+        out_specs=(vmem, vmem, vmem, vmem),
         scratch_shapes=[
             pltpu.VMEM((n_dp, n_col, depth, width), block.dtype),
             pltpu.VMEM((n_dp, n_col, depth, width), jnp.float32),
@@ -310,9 +293,16 @@
             pltpu.SemaphoreType.DMA((n_dp,)),
             pltpu.SemaphoreType.DMA((n_dp,)),
             pltpu.SemaphoreType.DMA((n_dp,)),
+            pltpu.VMEM((n, 8, 128), jnp.float32),
+            pltpu.VMEM((n_col,) + master.shape, jnp.float32),
+            pltpu.VMEM((n_col, master.shape[0], average.shape[1]), jnp.float32),
+            pltpu.SemaphoreType.DMA((n,)),
+            pltpu.SemaphoreType.DMA((n,)),
+            pltpu.SemaphoreType.DMA((n_col,)),
+            pltpu.SemaphoreType.DMA((n_col,)),
         ],
         compiler_params=pltpu.CompilerParams(collective_id=1, has_side_effects=True),
-    )(block, ln_part)
+    )(block, ln_part, master, first, second)
 
 
 def shards(
@@ -327,9 +317,8 @@
     ln_second,
     ln_average,
 ):
-    gradient, ln_gradient = reduce_blocks(grad_blocks[0], ln_grads[0])
-    clip_tile, block_master = finish(
-        gradient, ln_gradient, master, first_moment, second_moment, average
+    gradient, ln_gradient, clip_tile, block_master = reduce_blocks(
+        grad_blocks[0], ln_grads[0], master, first_moment, second_moment, average
     )
     clip_scale = clip_tile[0, 0]
     master_new, first_new, second_new = adam_step(

time: 88.7 us -> 84.6 us (0.954)
  Pallas kernels: 80.2 us -> 75.2 us
  other arithmetic: 5.45 us -> 6.4 us
    pallas_call x2 -> x1, Pallas kernels: 80.2 us -> 75.2 us  [reduce_blocks(): pl.pallas_call(functools.partial(reduce_kernel, n_dp, n_row, n_col), out_...]
    sub x1, other arithmetic: 2.12 us -> 3.11 us  [adam_step(): master_new = master - learn_rate * (direction + decay_weight * master)]
where the time goes in v7:
time: 84.6 us; the launch traced here: 84.3 us
  Pallas kernels  75.2 us (89%)
  other arithmetic  6.4 us (8%)
  local copies, waits for them, and re-layouts  1.92 us (2%)
    pallas_call x1, Pallas kernels, reduce_blocks(): pl.pallas_call(functools.partial(reduce_kernel, n_dp, n_row, n_col), out_...  75.2 us
    sub x1, other arithmetic, adam_step(): master_new = master - learn_rate * (direction + decay_weight * master)  3.11 us
    add x1, other arithmetic, shards(): average_new = ema_keep * average + (1.0 - ema_keep) * block_master  2.03 us

profile of v7, /device:TPU:1, one launch (start us, length us, event | category | flops | bytes accessed | tf_op | source)
XLA Modules:
  0.0 84.3 jit_solution(7364046102014671521)
XLA Ops:
  0.6 0.0 copy-start.3
  0.6 75.2 %shard_map.161 = (f32[128,1024]{1,0:T(8,128)}, f32[4,256]{1,0:T(4,128)}, f32[8,128]{1,0:T(8,128)}, f32[512,256]{1,0:T(8,128)}) custom-call(bf16[512,256]{1,0:T(8,128)(2,1)} %bitcast.3, bf16[4,256]{1,0:T(4,128)(2,1)} %bitcast.4, f32[128,1024]{1,0:T(8,128)} %m_ref.1, f32[128,1024]{1,0:T(8,128)} %f_ref.1, f32[128,1024]{1,0:T(8,128)} %s_ref.1), custom_call_target="tpu_custom_call" | custom-call | tf_op jit(solution)/shard_map/pallas_call | solution.py:276
  75.9 0.0 copy-done.3
  75.9 0.0 copy-start
  75.9 0.0 copy-start.1
  75.9 0.0 copy-start.2
  75.9 2.0 %multiply_add_fusion.1 = f32[512,256]{1,0:T(8,128)} fusion(f32[512,256]{1,0:T(8,128)} %get-tuple-element.12, f32[512,256]{1,0:T(8,128)S(1)} %copy-done.3), kind=kLoop, calls=%fused_computation.4 | loop fusion | flops 393216 | bytes 1572864 | tf_op jit(solution)/shard_map/add | solution.py:331
  78.0 1.2 %slice.3 = f32[1,1]{1,0:T(1,128)} slice(f32[8,128]{1,0:T(8,128)} %get-tuple-element.13), slice={[0:1], [0:1]} | slice | bytes 8 | tf_op jit(solution)/shard_map/slice | solution.py:323
  79.2 0.0 copy-done
  79.2 0.0 copy-done.1
  79.2 0.0 copy-done.2
  79.2 0.0 copy-start.5
  79.2 0.0 copy-start.6
  79.2 0.0 copy-start.7
  79.2 0.0 copy-start.8
  79.2 3.1 %multiply_subtract_fusion = (f32[128,1024]{1,0:T(8,128)}, f32[128,1024]{1,0:T(8,128)}, f32[128,1024]{1,0:T(8,128)}) fusion(f32[128,1024]{1,0:T(8,128)S(1)} %copy-done, f32[128,1024]{1,0:T(8,128)} %get-tuple-element.14, f32[]{:T(128)} %bitcast.2, f32[128,1024]{1,0:T(8,128)S(1)} %copy-done.1, f32[128,1024]{1,0:T(8,128)S(1)} %copy-done.2), kind=kLoop, calls=%fused_computation.2 | loop fusion | flops 2097152 | bytes 3670020 | tf_op jit(solution)/shard_map/sub | solution.py:36
  82.3 0.0 copy-start.4
  82.3 0.0 copy-done.5
  82.3 0.0 copy-done.6
  82.4 0.0 copy-done.7
  82.4 0.0 copy-done.8
  82.4 0.7 copy-done.4
  83.0 1.3 %multiply_add_fusion.2 = (f32[4,256]{1,0:T(4,128)}, f32[4,256]{1,0:T(4,128)}, f32[4,256]{1,0:T(4,128)}, f32[4,256]{1,0:T(4,128)}) fusion(f32[4,256]{1,0:T(4,128)S(1)} %copy-done.4, f32[4,256]{1,0:T(4,128)S(1)} %copy-done.5, f32[4,256]{1,0:T(4,128)S(1)} %copy-done.8, f32[]{:T(128)} %bitcast.2, f32[4,256]{1,0:T(4,128)S(1)} %copy-done.6, f32[4,256]{1,0:T(4,128)S(1)} %copy-done.7), kind=kLoop, calls=%fused_computation.7 | loop fusion | flops 19456 | bytes 36868 | tf_op jit(solution)/shard_map/add | solution.py:330
Async XLA Ops:
  0.6 75.2 %copy-start.3 = (f32[512,256]{1,0:T(8,128)S(1)}, f32[512,256]{1,0:T(8,128)}, u32[]{:S(2)}) copy-start(f32[512,256]{1,0:T(8,128)} %param.15) | copy-start | bytes 1572868
  75.9 3.3 %copy-start = (f32[128,1024]{1,0:T(8,128)S(1)}, f32[128,1024]{1,0:T(8,128)}, u32[]{:S(2)}) copy-start(f32[128,1024]{1,0:T(8,128)} %m_ref.1) | copy-start | bytes 1572868
  75.9 3.3 %copy-start.1 = (f32[128,1024]{1,0:T(8,128)S(1)}, f32[128,1024]{1,0:T(8,128)}, u32[]{:S(2)}) copy-start(f32[128,1024]{1,0:T(8,128)} %f_ref.1) | copy-start | bytes 1572868
  75.9 3.3 %copy-start.2 = (f32[128,1024]{1,0:T(8,128)S(1)}, f32[128,1024]{1,0:T(8,128)}, u32[]{:S(2)}) copy-start(f32[128,1024]{1,0:T(8,128)} %s_ref.1) | copy-start | bytes 1572868
  79.2 3.2 %copy-start.5 = (f32[4,256]{1,0:T(4,128)S(1)}, f32[4,256]{1,0:T(4,128)}, u32[]{:S(2)}) copy-start(f32[4,256]{1,0:T(4,128)} %param.16) | copy-start | bytes 12292
  79.2 3.2 %copy-start.6 = (f32[4,256]{1,0:T(4,128)S(1)}, f32[4,256]{1,0:T(4,128)}, u32[]{:S(2)}) copy-start(f32[4,256]{1,0:T(4,128)} %param.17) | copy-start | bytes 12292
  79.2 3.1 %copy-start.7 = (f32[4,256]{1,0:T(4,128)S(1)}, f32[4,256]{1,0:T(4,128)}, u32[]{:S(2)}) copy-start(f32[4,256]{1,0:T(4,128)} %param.18) | copy-start | bytes 12292
  79.2 3.1 %copy-start.8 = (f32[4,256]{1,0:T(4,128)S(1)}, f32[4,256]{1,0:T(4,128)}, u32[]{:S(2)}) copy-start(f32[4,256]{1,0:T(4,128)} %get-tuple-element.15) | copy-start | bytes 12292
  82.3 0.7 copy-start.4

commit v8 on v7

--- a/solution.py
+++ b/solution.py
@@ -305,6 +305,60 @@
     )(block, ln_part, master, first, second)
 
 
+def apply_kernel(c_ref, g_ref, m_ref, f_ref, s_ref, a_ref, b_ref, lg_ref, lm_ref, lf_ref, ls_ref,
+                 la_ref, a_out, m_out, f_out, s_out, lm_out, lf_out, ls_out, la_out,
+                 flat, block, small, sems):
+    clip_scale = c_ref[0:1, 0:1]
+    master_new, first_new, second_new = adam_step(
+        g_ref[...], clip_scale, f_ref[...], s_ref[...], m_ref[...], decay_rate
+    )
+    flat[0] = master_new
+    flat[1] = first_new
+    flat[2] = second_new
+    block[...] = ema_keep * a_ref[...] + (1.0 - ema_keep) * b_ref[...]
+    ln_master_new, ln_first_new, ln_second_new = adam_step(
+        lg_ref[...], clip_scale, lf_ref[...], ls_ref[...], lm_ref[...], 0.0
+    )
+    small[0] = ln_master_new
+    small[1] = ln_first_new
+    small[2] = ln_second_new
+    small[3] = ema_keep * la_ref[...] + (1.0 - ema_keep) * ln_master_new
+    copies = [
+        pltpu.make_async_copy(flat.at[0], m_out, sems.at[0]),
+        pltpu.make_async_copy(flat.at[1], f_out, sems.at[1]),
+        pltpu.make_async_copy(flat.at[2], s_out, sems.at[2]),
+        pltpu.make_async_copy(block, a_out, sems.at[3]),
+        pltpu.make_async_copy(small.at[0], lm_out, sems.at[4]),
+        pltpu.make_async_copy(small.at[1], lf_out, sems.at[5]),
+        pltpu.make_async_copy(small.at[2], ls_out, sems.at[6]),
+        pltpu.make_async_copy(small.at[3], la_out, sems.at[7]),
+    ]
+    for copy in copies:
+        copy.start()
+    for copy in copies:
+        copy.wait()
+
+
+def apply_update(clip_tile, gradient, master, first, second, average, block_master,
+                 ln_gradient, ln_master, ln_first, ln_second, ln_average):
+    vmem = pl.BlockSpec(memory_space=pltpu.VMEM)
+    anywhere = pl.BlockSpec(memory_space=pl.ANY)
+    outs = (average, master, first, second, ln_master, ln_first, ln_second, ln_average)
+    return pl.pallas_call(
+        apply_kernel,
+        out_shape=tuple(jax.ShapeDtypeStruct(x.shape, jnp.float32) for x in outs),
+        in_specs=[vmem] * 12,
+        out_specs=tuple([anywhere] * 8),
+        scratch_shapes=[
+            pltpu.VMEM((3,) + master.shape, jnp.float32),
+            pltpu.VMEM(average.shape, jnp.float32),
+            pltpu.VMEM((4,) + ln_master.shape, jnp.float32),
+            pltpu.SemaphoreType.DMA((8,)),
+        ],
+    )(clip_tile, gradient, master, first, second, average, block_master,
+      ln_gradient, ln_master, ln_first, ln_second, ln_average)
+
+
 def shards(
     grad_blocks,
     ln_grads,
@@ -320,15 +374,19 @@
     gradient, ln_gradient, clip_tile, block_master = reduce_blocks(
         grad_blocks[0], ln_grads[0], master, first_moment, second_moment, average
     )
-    clip_scale = clip_tile[0, 0]
-    master_new, first_new, second_new = adam_step(
-        gradient, clip_scale, first_moment, second_moment, master, decay_rate
-    )
-    ln_master_new, ln_first_new, ln_second_new = adam_step(
-        ln_gradient, clip_scale, ln_first, ln_second, ln_master, 0.0
-    )
-    ln_average_new = ema_keep * ln_average + (1.0 - ema_keep) * ln_master_new
-    average_new = ema_keep * average + (1.0 - ema_keep) * block_master
+    (
+        average_new,
+        master_new,
+        first_new,
+        second_new,
+        ln_master_new,
+        ln_first_new,
+        ln_second_new,
+        ln_average_new,
+    ) = apply_update(
+        clip_tile, gradient, master, first_moment, second_moment, average, block_master,
+        ln_gradient, ln_master, ln_first, ln_second, ln_average,
+    )
     return (
         average_new,
         master_new,

time: 84.6 us -> 80.1 us (0.947)
  other arithmetic: 6.4 us -> 0 us
  Pallas kernels: 75.2 us -> 79.3 us
  local copies, waits for them, and re-layouts: 1.92 us -> 0 us
    pallas_call x0 -> x1, Pallas kernels: none -> 4.15 us  [apply_update(): pl.pallas_call(apply_kernel, out_shape=tuple((jax.ShapeDtypeStruct(x.shap...]
    add x2 -> x0, other arithmetic: 3.28 us -> none  [the longest x1 2.03 us: shards(): average_new = ema_keep * average + (1.0 - ema_keep) * block_master]
    sub x1 -> x0, other arithmetic: 3.11 us -> none  [adam_step(): master_new = master - learn_rate * (direction + decay_weight * master)]
    slice x1 -> x0, local copies, waits for them, and re-layouts: 1.21 us -> none  [shards(): clip_scale = clip_tile[0, 0]]
where the time goes in v8:
time: 80.1 us; the launch traced here: 79.9 us
  Pallas kernels  79.3 us (99%)
    pallas_call x1, Pallas kernels, reduce_blocks(): pl.pallas_call(functools.partial(reduce_kernel, n_dp, n_row, n_col), out_...  75.1 us
    pallas_call x1, Pallas kernels, apply_update(): pl.pallas_call(apply_kernel, out_shape=tuple((jax.ShapeDtypeStruct(x.shap...  4.15 us

profile of v8, /device:TPU:1, one launch (start us, length us, event | category | flops | bytes accessed | tf_op | source)
XLA Modules:
  0.0 79.9 jit_solution(14921364282881247603)
XLA Ops:
  0.6 75.1 %shard_map.161 = (f32[128,1024]{1,0:T(8,128)}, f32[4,256]{1,0:T(4,128)}, f32[8,128]{1,0:T(8,128)}, f32[512,256]{1,0:T(8,128)}) custom-call(bf16[512,256]{1,0:T(8,128)(2,1)} %bitcast.2, bf16[4,256]{1,0:T(4,128)(2,1)} %bitcast.3, f32[128,1024]{1,0:T(8,128)} %m_ref.3, f32[128,1024]{1,0:T(8,128)} %f_ref.3, f32[128,1024]{1,0:T(8,128)} %s_ref.3), custom_call_target="tpu_custom_call" | custom-call | tf_op jit(solution)/shard_map/pallas_call | solution.py:276
  75.7 4.2 %shard_map.162 = (f32[512,256]{1,0:T(8,128)}, f32[128,1024]{1,0:T(8,128)}, f32[128,1024]{1,0:T(8,128)}, f32[128,1024]{1,0:T(8,128)}, f32[4,256]{1,0:T(4,128)}, /...) custom-call(f32[8,128]{1,0:T(8,128)} %get-tuple-element.12.c_ref, f32[128,1024]{1,0:T(8,128)} %get-tuple-element.13.g_ref, ...), custom_call_target="tpu_custom_call" | custom-call | tf_op jit(solution)/shard_map/pallas_call | solution.py:347

commit v9 on v8

--- a/solution.py
+++ b/solution.py
@@ -45,39 +45,12 @@
     return jnp.sum(gradient * gradient) + jnp.sum(ln_gradient * ln_gradient) / row_count
 
 
-def finish_part(n_row, n_col, g_ref, lg_ref, m_ref, f_ref, s_ref, c_out, b_out,
-                nbuf, mbuf, rbuf, n_send, n_recv, m_send, m_recv):
+def finish_part(n_col, g_ref, m_ref, f_ref, s_ref, c_out, b_out, norm_total,
+                mbuf, rbuf, m_send, m_recv):
     d = lax.axis_index("dp")
     r = lax.axis_index("row")
     c = lax.axis_index("col")
-    me = r * n_col + c
-    n = n_row * n_col
     g = g_ref[...]
-    lg = lg_ref[...]
-    part = jnp.sum(g * g) + jnp.sum(lg * lg) / float(n_row)
-    nbuf[me] = jnp.full(nbuf.shape[1:], part, jnp.float32)
-
-    def n_copy(j, peer, slot):
-        return pltpu.make_async_remote_copy(
-            src_ref=nbuf.at[slot],
-            dst_ref=nbuf.at[slot],
-            send_sem=n_send.at[j],
-            recv_sem=n_recv.at[slot],
-            device_id=(d, peer // n_col, peer % n_col),
-            device_id_type=MESH,
-        )
-
-    copies = []
-    for j in range(1, n):
-        copy = n_copy(j, lax.rem(me + j, n), me)
-        copy.start()
-        copies.append(copy)
-    for j in range(1, n):
-        sender = lax.rem(me + n - j, n)
-        n_copy(j, sender, sender).wait_recv()
-    for copy in copies:
-        copy.wait_send()
-    norm_total = jnp.sum(nbuf[...], axis=0)[0:1, 0:1]
     clip_scale = clip_factor(norm_total)
     c_out[...] = jnp.broadcast_to(clip_scale, c_out.shape)
     master_new, _, _ = adam_step(g, clip_scale, f_ref[...], s_ref[...], m_ref[...], decay_rate)
@@ -113,7 +86,7 @@
 def reduce_kernel(n_dp, n_row, n_col, g_ref, ln_ref, m_ref, f_ref, s_ref,
                   g_out, ln_out, c_out, b_out, rs_buf, ag_buf, ln_buf,
                   rs_send, rs_recv, ag_send, ag_recv, ln_send, ln_recv,
-                  nbuf, mbuf, rbuf, n_send, n_recv, m_send, m_recv):
+                  nbuf, mbuf, rbuf, n_send, n_recv, m_send, m_recv, pbuf, p_send, p_recv):
     d = lax.axis_index("dp")
     r = lax.axis_index("row")
     c = lax.axis_index("col")
@@ -198,6 +171,22 @@
         return carry
 
     lax.fori_loop(1, n, wait_rs, 0)
+    def wait_ln(j, carry):
+        src = lax.rem(d + j, n_dp)
+        pltpu.make_async_remote_copy(
+            src_ref=ln_ref,
+            dst_ref=ln_buf.at[src],
+            send_sem=ln_send.at[j],
+            recv_sem=ln_recv.at[src],
+            device_id=(src, r, c),
+            device_id_type=MESH,
+        ).wait_recv()
+        ln_copy(j).wait_send()
+        return carry
+
+    lax.fori_loop(1, n_dp, wait_ln, 0)
+    ln_out[...] = jnp.sum(ln_buf[...].astype(jnp.float32), axis=0)
+
     ag_buf[d] = jnp.sum(rs_buf[...].astype(jnp.float32), axis=0)
 
     def ag_copy(slot, j, peer):
@@ -213,11 +202,35 @@
     def arrive(slot):
         ag_copy(slot, 0, slot).wait_recv()
 
+    n_rc = n_row * n_col
+    me_rc = r * n_col + c
+
+    def n_copy(j, peer, slot):
+        return pltpu.make_async_remote_copy(
+            src_ref=nbuf.at[slot],
+            dst_ref=nbuf.at[slot],
+            send_sem=n_send.at[j],
+            recv_sem=n_recv.at[slot],
+            device_id=(d, peer // n_col, peer % n_col),
+            device_id_type=MESH,
+        )
+
+    def p_copy(j, peer, slot):
+        return pltpu.make_async_remote_copy(
+            src_ref=pbuf.at[slot],
+            dst_ref=pbuf.at[slot],
+            send_sem=p_send.at[j],
+            recv_sem=p_recv.at[slot],
+            device_id=(peer, r, c),
+            device_id_type=MESH,
+        )
+
     reach = 3
     n_right = n_dp // 2
     n_left = n_dp - 1 - n_right
     sends = []
     waited = set()
+    n_copies = []
     for leg in range(0, n_right, reach):
         for sign, span in ((1, n_right), (-1, n_left)):
             if leg >= span:
@@ -232,36 +245,48 @@
                 copy = ag_copy(slot, len(sends), peer)
                 copy.start()
                 sends.append(copy)
-
-    def wait_ln(j, carry):
-        src = lax.rem(d + j, n_dp)
-        pltpu.make_async_remote_copy(
-            src_ref=ln_ref,
-            dst_ref=ln_buf.at[src],
-            send_sem=ln_send.at[j],
-            recv_sem=ln_recv.at[src],
-            device_id=(src, r, c),
-            device_id_type=MESH,
-        ).wait_recv()
-        ln_copy(j).wait_send()
-        return carry
-
-    lax.fori_loop(1, n_dp, wait_ln, 0)
-    ln_out[...] = jnp.sum(ln_buf[...].astype(jnp.float32), axis=0)
-
+        if leg == 0:
+            lg = ln_out[...]
+            own = ag_buf[d]
+            part = jnp.sum(own * own) + (d == 0).astype(jnp.float32) * (
+                jnp.sum(lg * lg) / float(n_row)
+            )
+            nbuf[me_rc] = jnp.full(nbuf.shape[1:], part, jnp.float32)
+            for j in range(1, n_rc):
+                copy = n_copy(j, lax.rem(me_rc + j, n_rc), me_rc)
+                copy.start()
+                n_copies.append(copy)
+
+    for j in range(1, n_rc):
+        sender = lax.rem(me_rc + n_rc - j, n_rc)
+        n_copy(j, sender, sender).wait_recv()
+    for copy in n_copies:
+        copy.wait_send()
+    pbuf[d] = jnp.sum(nbuf[...], axis=0)
+    p_copies = []
+    for j in range(1, n_dp):
+        copy = p_copy(j, lax.rem(d + j, n_dp), d)
+        copy.start()
+        p_copies.append(copy)
     for back in range(1, n_dp):
         if back not in waited:
             arrive(lax.rem(d + back, n_dp))
     for copy in sends:
         copy.wait_send()
+    for j in range(1, n_dp):
+        sender = lax.rem(d + n_dp - j, n_dp)
+        p_copy(j, sender, sender).wait_recv()
+    for copy in p_copies:
+        copy.wait_send()
+    norm_total = jnp.sum(pbuf[...], axis=0)[0:1, 0:1]
     for k in range(n_dp):
         for q in range(n_col):
             g_out[
                 pl.ds((k // halves) * depth, depth),
                 pl.ds(q * halves * width + (k % halves) * width, width),
             ] = ag_buf[k, q]
-    finish_part(n_row, n_col, g_out, ln_out, m_ref, f_ref, s_ref, c_out, b_out,
-                nbuf, mbuf, rbuf, n_send, n_recv, m_send, m_recv)
+    finish_part(n_col, g_out, m_ref, f_ref, s_ref, c_out, b_out, norm_total,
+                mbuf, rbuf, m_send, m_recv)
 
 
 def reduce_blocks(block, ln_part, master, first, second, average):
@@ -300,6 +325,9 @@
             pltpu.SemaphoreType.DMA((n,)),
             pltpu.SemaphoreType.DMA((n_col,)),
             pltpu.SemaphoreType.DMA((n_col,)),
+            pltpu.VMEM((n_dp, 8, 128), jnp.float32),
+            pltpu.SemaphoreType.DMA((n_dp,)),
+            pltpu.SemaphoreType.DMA((n_dp,)),
         ],
         compiler_params=pltpu.CompilerParams(collective_id=1, has_side_effects=True),
     )(block, ln_part, master, first, second)

time: 80.1 us -> 74.6 us (0.931)
  the two profiles are of different devices: /device:TPU:1 before, /device:TPU:8 now
where the time goes in v9:
time: 74.6 us; the launch traced here: 74.4 us
  Pallas kernels  73.8 us (99%)
    pallas_call x1, Pallas kernels, reduce_blocks(): pl.pallas_call(functools.partial(reduce_kernel, n_dp, n_row, n_col), out_...  69.6 us
    pallas_call x1, Pallas kernels, apply_update(): pl.pallas_call(apply_kernel, out_shape=tuple((jax.ShapeDtypeStruct(x.shap...  4.15 us

profile of v9, /device:TPU:8, one launch (start us, length us, event | category | flops | bytes accessed | tf_op | source)
XLA Modules:
  0.0 74.4 jit_solution(17515250528291269222)
XLA Ops:
  0.6 69.6 %shard_map.161 = (f32[128,1024]{1,0:T(8,128)}, f32[4,256]{1,0:T(4,128)}, f32[8,128]{1,0:T(8,128)}, f32[512,256]{1,0:T(8,128)}) custom-call(bf16[512,256]{1,0:T(8,128)(2,1)} %bitcast.2, bf16[4,256]{1,0:T(4,128)(2,1)} %bitcast.3, f32[128,1024]{1,0:T(8,128)} %m_ref.3, f32[128,1024]{1,0:T(8,128)} %f_ref.3, f32[128,1024]{1,0:T(8,128)} %s_ref.3), custom_call_target="tpu_custom_call" | custom-call | tf_op jit(solution)/shard_map/pallas_call | solution.py:301
  70.3 4.2 %shard_map.162 = (f32[512,256]{1,0:T(8,128)}, f32[128,1024]{1,0:T(8,128)}, f32[128,1024]{1,0:T(8,128)}, f32[128,1024]{1,0:T(8,128)}, f32[4,256]{1,0:T(4,128)}, /...) custom-call(f32[8,128]{1,0:T(8,128)} %get-tuple-element.12.c_ref, f32[128,1024]{1,0:T(8,128)} %get-tuple-element.13.g_ref, ...), custom_call_target="tpu_custom_call" | custom-call | tf_op jit(solution)/shard_map/pallas_call | solution.py:375

commit v10 on v9

--- a/solution.py
+++ b/solution.py
@@ -225,7 +225,7 @@
             device_id_type=MESH,
         )
 
-    reach = 3
+    reach = 4
     n_right = n_dp // 2
     n_left = n_dp - 1 - n_right
     sends = []

time: 74.6 us -> 76.3 us (1.023)
  the two profiles are of different devices: /device:TPU:8 before, /device:TPU:16 now
where the time goes in v10:
time: 76.3 us; the launch traced here: 76.2 us
  Pallas kernels  75.5 us (99%)
    pallas_call x1, Pallas kernels, reduce_blocks(): pl.pallas_call(functools.partial(reduce_kernel, n_dp, n_row, n_col), out_...  71.4 us
    pallas_call x1, Pallas kernels, apply_update(): pl.pallas_call(apply_kernel, out_shape=tuple((jax.ShapeDtypeStruct(x.shap...  4.15 us

profile of v10, /device:TPU:16, one launch (start us, length us, event | category | flops | bytes accessed | tf_op | source)
XLA Modules:
  0.0 76.2 jit_solution(6782306820250021732)
XLA Ops:
  0.6 71.4 %shard_map.161 = (f32[128,1024]{1,0:T(8,128)}, f32[4,256]{1,0:T(4,128)}, f32[8,128]{1,0:T(8,128)}, f32[512,256]{1,0:T(8,128)}) custom-call(bf16[512,256]{1,0:T(8,128)(2,1)} %bitcast.2, bf16[4,256]{1,0:T(4,128)(2,1)} %bitcast.3, f32[128,1024]{1,0:T(8,128)} %m_ref.3, f32[128,1024]{1,0:T(8,128)} %f_ref.3, f32[128,1024]{1,0:T(8,128)} %s_ref.3), custom_call_target="tpu_custom_call" | custom-call | tf_op jit(solution)/shard_map/pallas_call | solution.py:301
  72.0 4.2 %shard_map.162 = (f32[512,256]{1,0:T(8,128)}, f32[128,1024]{1,0:T(8,128)}, f32[128,1024]{1,0:T(8,128)}, f32[128,1024]{1,0:T(8,128)}, f32[4,256]{1,0:T(4,128)}, /...) custom-call(f32[8,128]{1,0:T(8,128)} %get-tuple-element.12.c_ref, f32[128,1024]{1,0:T(8,128)} %get-tuple-element.13.g_ref, ...), custom_call_target="tpu_custom_call" | custom-call | tf_op jit(solution)/shard_map/pallas_call | solution.py:375

commit v11 on v10

--- a/solution.py
+++ b/solution.py
@@ -225,7 +225,7 @@
             device_id_type=MESH,
         )
 
-    reach = 4
+    reach = 2
     n_right = n_dp // 2
     n_left = n_dp - 1 - n_right
     sends = []

time: 76.3 us -> 75.5 us (0.990)
  the two profiles are of different devices: /device:TPU:16 before, /device:TPU:8 now
where the time goes in v11:
time: 75.5 us; the launch traced here: 75.3 us
  Pallas kernels  74.7 us (99%)
    pallas_call x1, Pallas kernels, reduce_blocks(): pl.pallas_call(functools.partial(reduce_kernel, n_dp, n_row, n_col), out_...  70.5 us
    pallas_call x1, Pallas kernels, apply_update(): pl.pallas_call(apply_kernel, out_shape=tuple((jax.ShapeDtypeStruct(x.shap...  4.15 us

profile of v11, /device:TPU:8, one launch (start us, length us, event | category | flops | bytes accessed | tf_op | source)
XLA Modules:
  0.0 75.3 jit_solution(3645336007512900879)
XLA Ops:
  0.6 70.5 %shard_map.161 = (f32[128,1024]{1,0:T(8,128)}, f32[4,256]{1,0:T(4,128)}, f32[8,128]{1,0:T(8,128)}, f32[512,256]{1,0:T(8,128)}) custom-call(bf16[512,256]{1,0:T(8,128)(2,1)} %bitcast.2, bf16[4,256]{1,0:T(4,128)(2,1)} %bitcast.3, f32[128,1024]{1,0:T(8,128)} %m_ref.3, f32[128,1024]{1,0:T(8,128)} %f_ref.3, f32[128,1024]{1,0:T(8,128)} %s_ref.3), custom_call_target="tpu_custom_call" | custom-call | tf_op jit(solution)/shard_map/pallas_call | solution.py:301
  71.2 4.2 %shard_map.162 = (f32[512,256]{1,0:T(8,128)}, f32[128,1024]{1,0:T(8,128)}, f32[128,1024]{1,0:T(8,128)}, f32[128,1024]{1,0:T(8,128)}, f32[4,256]{1,0:T(4,128)}, /...) custom-call(f32[8,128]{1,0:T(8,128)} %get-tuple-element.12.c_ref, f32[128,1024]{1,0:T(8,128)} %get-tuple-element.13.g_ref, ...), custom_call_target="tpu_custom_call" | custom-call | tf_op jit(solution)/shard_map/pallas_call | solution.py:375

commit v12 on v9

--- a/solution.py
+++ b/solution.py
@@ -50,16 +50,20 @@
     d = lax.axis_index("dp")
     r = lax.axis_index("row")
     c = lax.axis_index("col")
-    g = g_ref[...]
     clip_scale = clip_factor(norm_total)
     c_out[...] = jnp.broadcast_to(clip_scale, c_out.shape)
-    master_new, _, _ = adam_step(g, clip_scale, f_ref[...], s_ref[...], m_ref[...], decay_rate)
-    mbuf[c] = master_new
     width = b_out.shape[1]
 
+    def chunk(peer):
+        cols = pl.ds(pl.multiple_of(peer * width, width), width)
+        master_new, _, _ = adam_step(
+            g_ref[:, cols], clip_scale, f_ref[:, cols], s_ref[:, cols], m_ref[:, cols], decay_rate
+        )
+        return master_new
+
     def m_copy(j, peer, slot):
         return pltpu.make_async_remote_copy(
-            src_ref=mbuf.at[c, :, pl.ds(pl.multiple_of(peer * width, width), width)],
+            src_ref=mbuf.at[peer],
             dst_ref=rbuf.at[slot],
             send_sem=m_send.at[j],
             recv_sem=m_recv.at[slot],
@@ -69,10 +73,12 @@
 
     copies = []
     for j in range(1, n_col):
-        copy = m_copy(j, lax.rem(c + j, n_col), c)
+        peer = lax.rem(c + j, n_col)
+        mbuf[peer] = chunk(peer)
+        copy = m_copy(j, peer, c)
         copy.start()
         copies.append(copy)
-    rbuf[c] = mbuf[c, :, pl.ds(pl.multiple_of(c * width, width), width)]
+    rbuf[c] = chunk(c)
     for j in range(1, n_col):
         sender = lax.rem(c + n_col - j, n_col)
         m_copy(j, sender, sender).wait_recv()
@@ -319,7 +325,7 @@
             pltpu.SemaphoreType.DMA((n_dp,)),
             pltpu.SemaphoreType.DMA((n_dp,)),
             pltpu.VMEM((n, 8, 128), jnp.float32),
-            pltpu.VMEM((n_col,) + master.shape, jnp.float32),
+            pltpu.VMEM((n_col, master.shape[0], average.shape[1]), jnp.float32),
             pltpu.VMEM((n_col, master.shape[0], average.shape[1]), jnp.float32),
             pltpu.SemaphoreType.DMA((n,)),
             pltpu.SemaphoreType.DMA((n,)),
@@ -343,7 +349,17 @@
     flat[0] = master_new
     flat[1] = first_new
     flat[2] = second_new
+    copies = [
+        pltpu.make_async_copy(flat.at[0], m_out, sems.at[0]),
+        pltpu.make_async_copy(flat.at[1], f_out, sems.at[1]),
+        pltpu.make_async_copy(flat.at[2], s_out, sems.at[2]),
+    ]
+    for copy in copies:
+        copy.start()
     block[...] = ema_keep * a_ref[...] + (1.0 - ema_keep) * b_ref[...]
+    copy = pltpu.make_async_copy(block, a_out, sems.at[3])
+    copy.start()
+    copies.append(copy)
     ln_master_new, ln_first_new, ln_second_new = adam_step(
         lg_ref[...], clip_scale, lf_ref[...], ls_ref[...], lm_ref[...], 0.0
     )
@@ -351,18 +367,10 @@
     small[1] = ln_first_new
     small[2] = ln_second_new
     small[3] = ema_keep * la_ref[...] + (1.0 - ema_keep) * ln_master_new
-    copies = [
-        pltpu.make_async_copy(flat.at[0], m_out, sems.at[0]),
-        pltpu.make_async_copy(flat.at[1], f_out, sems.at[1]),
-        pltpu.make_async_copy(flat.at[2], s_out, sems.at[2]),
-        pltpu.make_async_copy(block, a_out, sems.at[3]),
-        pltpu.make_async_copy(small.at[0], lm_out, sems.at[4]),
-        pltpu.make_async_copy(small.at[1], lf_out, sems.at[5]),
-        pltpu.make_async_copy(small.at[2], ls_out, sems.at[6]),
-        pltpu.make_async_copy(small.at[3], la_out, sems.at[7]),
-    ]
-    for copy in copies:
+    for i, out in enumerate((lm_out, lf_out, ls_out, la_out)):
+        copy = pltpu.make_async_copy(small.at[i], out, sems.at[4 + i])
         copy.start()
+        copies.append(copy)
     for copy in copies:
         copy.wait()
 

time: 74.6 us -> 73.9 us (level)
  no operation moved by 1% of the time
where the time goes in v12:
time: 73.9 us; the launch traced here: 73.8 us
  Pallas kernels  73.1 us (99%)
    pallas_call x1, Pallas kernels, reduce_blocks(): pl.pallas_call(functools.partial(reduce_kernel, n_dp, n_row, n_col), out_...  69 us
    pallas_call x1, Pallas kernels, apply_update(): pl.pallas_call(apply_kernel, out_shape=tuple((jax.ShapeDtypeStruct(x.shap...  4.15 us

profile of v12, /device:TPU:8, one launch (start us, length us, event | category | flops | bytes accessed | tf_op | source)
XLA Modules:
  0.0 73.8 jit_solution(12485951478989476454)
XLA Ops:
  0.6 69.0 %shard_map.161 = (f32[128,1024]{1,0:T(8,128)}, f32[4,256]{1,0:T(4,128)}, f32[8,128]{1,0:T(8,128)}, f32[512,256]{1,0:T(8,128)}) custom-call(bf16[512,256]{1,0:T(8,128)(2,1)} %bitcast.2, bf16[4,256]{1,0:T(4,128)(2,1)} %bitcast.3, f32[128,1024]{1,0:T(8,128)} %m_ref.3, f32[128,1024]{1,0:T(8,128)} %f_ref.3, f32[128,1024]{1,0:T(8,128)} %s_ref.3), custom_call_target="tpu_custom_call" | custom-call | tf_op jit(solution)/shard_map/pallas_call | solution.py:307
  69.6 4.2 %shard_map.162 = (f32[512,256]{1,0:T(8,128)}, f32[128,1024]{1,0:T(8,128)}, f32[128,1024]{1,0:T(8,128)}, f32[128,1024]{1,0:T(8,128)}, f32[4,256]{1,0:T(4,128)}, /...) custom-call(f32[8,128]{1,0:T(8,128)} %get-tuple-element.12.c_ref, f32[128,1024]{1,0:T(8,128)} %get-tuple-element.13.g_ref, ...), custom_call_target="tpu_custom_call" | custom-call | tf_op jit(solution)/shard_map/pallas_call | solution.py:383

commit v13 on v12

--- a/solution.py
+++ b/solution.py
@@ -129,13 +129,18 @@
         return g_ref.at[rows, cols]
 
     def rs_copy(j):
-        peer = lax.rem(me + j, n)
-        return pltpu.make_async_remote_copy(
-            src_ref=piece(peer // n_col, peer % n_col),
+        zi = j // n_col
+        half = n_dp // 2
+        size = half - (zi + 1) // 2
+        below = (1 - zi % 2) * ((zi + n_dp - 1) // n_dp)
+        k = lax.rem(d + size * (1 - 2 * below) + n_dp, n_dp)
+        q = lax.rem(c + (j + 1) % n_col, n_col)
+        return pltpu.make_async_remote_copy(
+            src_ref=piece(k, q),
             dst_ref=rs_buf.at[d, c],
             send_sem=rs_send.at[j],
             recv_sem=rs_recv.at[me],
-            device_id=(peer // n_col, r, peer % n_col),
+            device_id=(k, r, q),
             device_id_type=MESH,
         )
 
@@ -158,7 +163,7 @@
         ln_copy(j).start()
         return carry
 
-    lax.fori_loop(1, n, start_rs, 0)
+    lax.fori_loop(0, n - 1, start_rs, 0)
     lax.fori_loop(1, n_dp, start_ln, 0)
     rs_buf[d, c] = piece(d, c)[...]
     ln_buf[d] = ln_ref[...]
@@ -173,7 +178,7 @@
             device_id=(src // n_col, r, src % n_col),
             device_id_type=MESH,
         ).wait_recv()
-        rs_copy(j).wait_send()
+        rs_copy(j - 1).wait_send()
         return carry
 
     lax.fori_loop(1, n, wait_rs, 0)

time: 73.9 us -> 74 us (level)
  the two profiles are of different devices: /device:TPU:8 before, /device:TPU:6 now
where the time goes in v13:
time: 74 us; the launch traced here: 73.9 us
  Pallas kernels  73.2 us (99%)
    pallas_call x1, Pallas kernels, reduce_blocks(): pl.pallas_call(functools.partial(reduce_kernel, n_dp, n_row, n_col), out_...  69.1 us
    pallas_call x1, Pallas kernels, apply_update(): pl.pallas_call(apply_kernel, out_shape=tuple((jax.ShapeDtypeStruct(x.shap...  4.15 us

profile of v13, /device:TPU:6, one launch (start us, length us, event | category | flops | bytes accessed | tf_op | source)
XLA Modules:
  0.0 73.9 jit_solution(14492207092994395572)
XLA Ops:
  0.6 69.1 %shard_map.161 = (f32[128,1024]{1,0:T(8,128)}, f32[4,256]{1,0:T(4,128)}, f32[8,128]{1,0:T(8,128)}, f32[512,256]{1,0:T(8,128)}) custom-call(bf16[512,256]{1,0:T(8,128)(2,1)} %bitcast.2, bf16[4,256]{1,0:T(4,128)(2,1)} %bitcast.3, f32[128,1024]{1,0:T(8,128)} %m_ref.3, f32[128,1024]{1,0:T(8,128)} %f_ref.3, f32[128,1024]{1,0:T(8,128)} %s_ref.3), custom_call_target="tpu_custom_call" | custom-call | tf_op jit(solution)/shard_map/pallas_call | solution.py:312
  69.7 4.2 %shard_map.162 = (f32[512,256]{1,0:T(8,128)}, f32[128,1024]{1,0:T(8,128)}, f32[128,1024]{1,0:T(8,128)}, f32[128,1024]{1,0:T(8,128)}, f32[4,256]{1,0:T(4,128)}, /...) custom-call(f32[8,128]{1,0:T(8,128)} %get-tuple-element.12.c_ref, f32[128,1024]{1,0:T(8,128)} %get-tuple-element.13.g_ref, ...), custom_call_target="tpu_custom_call" | custom-call | tf_op jit(solution)/shard_map/pallas_call | solution.py:388

commit v14 on v12

--- a/solution.py
+++ b/solution.py
@@ -121,7 +121,6 @@
         return carry
 
     lax.fori_loop(0, (n_row - 1) * n_col, greet_row, 0)
-    pl.semaphore_wait(barrier, n - 1 + (n_row - 1) * n_col)
 
     def piece(k, q):
         rows = pl.ds(pl.multiple_of(q * quarter + (k // halves) * depth, depth), depth)
@@ -158,10 +157,11 @@
         ln_copy(j).start()
         return carry
 
-    lax.fori_loop(1, n, start_rs, 0)
-    lax.fori_loop(1, n_dp, start_ln, 0)
     rs_buf[d, c] = piece(d, c)[...]
     ln_buf[d] = ln_ref[...]
+    pl.semaphore_wait(barrier, n - 1 + (n_row - 1) * n_col)
+    lax.fori_loop(1, n_dp, start_ln, 0)
+    lax.fori_loop(1, n, start_rs, 0)
 
     def wait_rs(j, carry):
         src = lax.rem(me + j, n)

time: 73.9 us -> 74.9 us (1.014)
  the two profiles are of different devices: /device:TPU:8 before, /device:TPU:16 now
where the time goes in v14:
time: 74.9 us; the launch traced here: 74.8 us
  Pallas kernels  74.1 us (99%)
    pallas_call x1, Pallas kernels, reduce_blocks(): pl.pallas_call(functools.partial(reduce_kernel, n_dp, n_row, n_col), out_...  70 us
    pallas_call x1, Pallas kernels, apply_update(): pl.pallas_call(apply_kernel, out_shape=tuple((jax.ShapeDtypeStruct(x.shap...  4.15 us

profile of v14, /device:TPU:16, one launch (start us, length us, event | category | flops | bytes accessed | tf_op | source)
XLA Modules:
  0.0 74.8 jit_solution(8106507666456482837)
XLA Ops:
  0.6 70.0 %shard_map.161 = (f32[128,1024]{1,0:T(8,128)}, f32[4,256]{1,0:T(4,128)}, f32[8,128]{1,0:T(8,128)}, f32[512,256]{1,0:T(8,128)}) custom-call(bf16[512,256]{1,0:T(8,128)(2,1)} %bitcast.2, bf16[4,256]{1,0:T(4,128)(2,1)} %bitcast.3, f32[128,1024]{1,0:T(8,128)} %m_ref.3, f32[128,1024]{1,0:T(8,128)} %f_ref.3, f32[128,1024]{1,0:T(8,128)} %s_ref.3), custom_call_target="tpu_custom_call" | custom-call | tf_op jit(solution)/shard_map/pallas_call | solution.py:307
  70.6 4.2 %shard_map.162 = (f32[512,256]{1,0:T(8,128)}, f32[128,1024]{1,0:T(8,128)}, f32[128,1024]{1,0:T(8,128)}, f32[128,1024]{1,0:T(8,128)}, f32[4,256]{1,0:T(4,128)}, /...) custom-call(f32[8,128]{1,0:T(8,128)} %get-tuple-element.12.c_ref, f32[128,1024]{1,0:T(8,128)} %get-tuple-element.13.g_ref, ...), custom_call_target="tpu_custom_call" | custom-call | tf_op jit(solution)/shard_map/pallas_call | solution.py:383

commit v15 on v12

--- a/solution.py
+++ b/solution.py
@@ -340,57 +340,38 @@
 
 
 def apply_kernel(c_ref, g_ref, m_ref, f_ref, s_ref, a_ref, b_ref, lg_ref, lm_ref, lf_ref, ls_ref,
-                 la_ref, a_out, m_out, f_out, s_out, lm_out, lf_out, ls_out, la_out,
-                 flat, block, small, sems):
+                 la_ref, a_out, m_out, f_out, s_out, lm_out, lf_out, ls_out, la_out):
     clip_scale = c_ref[0:1, 0:1]
     master_new, first_new, second_new = adam_step(
         g_ref[...], clip_scale, f_ref[...], s_ref[...], m_ref[...], decay_rate
     )
-    flat[0] = master_new
-    flat[1] = first_new
-    flat[2] = second_new
-    copies = [
-        pltpu.make_async_copy(flat.at[0], m_out, sems.at[0]),
-        pltpu.make_async_copy(flat.at[1], f_out, sems.at[1]),
-        pltpu.make_async_copy(flat.at[2], s_out, sems.at[2]),
-    ]
-    for copy in copies:
-        copy.start()
-    block[...] = ema_keep * a_ref[...] + (1.0 - ema_keep) * b_ref[...]
-    copy = pltpu.make_async_copy(block, a_out, sems.at[3])
-    copy.start()
-    copies.append(copy)
+    m_out[...] = master_new
+    f_out[...] = first_new
+    s_out[...] = second_new
+    a_out[...] = ema_keep * a_ref[...] + (1.0 - ema_keep) * b_ref[...]
     ln_master_new, ln_first_new, ln_second_new = adam_step(
         lg_ref[...], clip_scale, lf_ref[...], ls_ref[...], lm_ref[...], 0.0
     )
-    small[0] = ln_master_new
-    small[1] = ln_first_new
-    small[2] = ln_second_new
-    small[3] = ema_keep * la_ref[...] + (1.0 - ema_keep) * ln_master_new
-    for i, out in enumerate((lm_out, lf_out, ls_out, la_out)):
-        copy = pltpu.make_async_copy(small.at[i], out, sems.at[4 + i])
-        copy.start()
-        copies.append(copy)
-    for copy in copies:
-        copy.wait()
+    lm_out[...] = ln_master_new
+    lf_out[...] = ln_first_new
+    ls_out[...] = ln_second_new
+    la_out[...] = ema_keep * la_ref[...] + (1.0 - ema_keep) * ln_master_new
 
 
 def apply_update(clip_tile, gradient, master, first, second, average, block_master,
                  ln_gradient, ln_master, ln_first, ln_second, ln_average):
-    vmem = pl.BlockSpec(memory_space=pltpu.VMEM)
-    anywhere = pl.BlockSpec(memory_space=pl.ANY)
+    steps = 4
+    flat = pl.BlockSpec((master.shape[0] // steps, master.shape[1]), lambda i: (i, 0))
+    block = pl.BlockSpec((average.shape[0] // steps, average.shape[1]), lambda i: (i, 0))
+    whole = pl.BlockSpec(clip_tile.shape, lambda i: (0, 0))
+    small = pl.BlockSpec(ln_master.shape, lambda i: (0, 0))
     outs = (average, master, first, second, ln_master, ln_first, ln_second, ln_average)
     return pl.pallas_call(
         apply_kernel,
         out_shape=tuple(jax.ShapeDtypeStruct(x.shape, jnp.float32) for x in outs),
-        in_specs=[vmem] * 12,
-        out_specs=tuple([anywhere] * 8),
-        scratch_shapes=[
-            pltpu.VMEM((3,) + master.shape, jnp.float32),
-            pltpu.VMEM(average.shape, jnp.float32),
-            pltpu.VMEM((4,) + ln_master.shape, jnp.float32),
-            pltpu.SemaphoreType.DMA((8,)),
-        ],
+        grid=(steps,),
+        in_specs=[whole, flat, flat, flat, flat, block, block, small, small, small, small, small],
+        out_specs=(block, flat, flat, flat, small, small, small, small),
     )(clip_tile, gradient, master, first, second, average, block_master,
       ln_gradient, ln_master, ln_first, ln_second, ln_average)
 

time: 73.9 us -> 74.2 us (level)
  no operation moved by 1% of the time
where the time goes in v15:
time: 74.2 us; the launch traced here: 73.9 us
  Pallas kernels  73.3 us (99%)
    pallas_call x1, Pallas kernels, reduce_blocks(): pl.pallas_call(functools.partial(reduce_kernel, n_dp, n_row, n_col), out_...  69 us
    pallas_call x1, Pallas kernels, apply_update(): pl.pallas_call(apply_kernel, out_shape=tuple((jax.ShapeDtypeStruct(x.shap...  4.3 us

profile of v15, /device:TPU:8, one launch (start us, length us, event | category | flops | bytes accessed | tf_op | source)
XLA Modules:
  0.0 73.9 jit_solution(4150328350515248768)
XLA Ops:
  0.6 69.0 %shard_map.161 = (f32[128,1024]{1,0:T(8,128)}, f32[4,256]{1,0:T(4,128)}, f32[8,128]{1,0:T(8,128)}, f32[512,256]{1,0:T(8,128)}) custom-call(bf16[512,256]{1,0:T(8,128)(2,1)} %bitcast.2, bf16[4,256]{1,0:T(4,128)(2,1)} %bitcast.3, f32[128,1024]{1,0:T(8,128)} %m_ref.3, f32[128,1024]{1,0:T(8,128)} %f_ref.3, f32[128,1024]{1,0:T(8,128)} %s_ref.3), custom_call_target="tpu_custom_call" | custom-call | tf_op jit(solution)/shard_map/pallas_call | solution.py:307
  69.6 4.3 %shard_map.162 = (f32[512,256]{1,0:T(8,128)}, f32[128,1024]{1,0:T(8,128)}, f32[128,1024]{1,0:T(8,128)}, f32[128,1024]{1,0:T(8,128)}, f32[4,256]{1,0:T(4,128)}, /...) custom-call(f32[8,128]{1,0:T(8,128)} %get-tuple-element.12.c_ref, f32[128,1024]{1,0:T(8,128)} %get-tuple-element.13.g_ref, ...), custom_call_target="tpu_custom_call" | custom-call | tf_op jit(solution)/shard_map/pallas_call | solution.py:369

commit v16 on v12

--- a/solution.py
+++ b/solution.py
@@ -114,14 +114,12 @@
     lax.fori_loop(1, n, greet, 0)
 
     def greet_row(j, carry):
-        peer = lax.rem(r + 1 + j // n_col, n_row)
-        pl.semaphore_signal(
-            barrier, inc=1, device_id=(d, peer, j % n_col), device_id_type=MESH
-        )
-        return carry
-
-    lax.fori_loop(0, (n_row - 1) * n_col, greet_row, 0)
-    pl.semaphore_wait(barrier, n - 1 + (n_row - 1) * n_col)
+        peer = lax.rem(r + 1 + j, n_row)
+        pl.semaphore_signal(barrier, inc=1, device_id=(d, peer, c), device_id_type=MESH)
+        return carry
+
+    lax.fori_loop(0, n_row - 1, greet_row, 0)
+    pl.semaphore_wait(barrier, n - 1 + n_row - 1)
 
     def piece(k, q):
         rows = pl.ds(pl.multiple_of(q * quarter + (k // halves) * depth, depth), depth)
@@ -211,13 +209,23 @@
     n_rc = n_row * n_col
     me_rc = r * n_col + c
 
-    def n_copy(j, peer, slot):
+    def col_copy(j, peer, slot):
         return pltpu.make_async_remote_copy(
             src_ref=nbuf.at[slot],
             dst_ref=nbuf.at[slot],
             send_sem=n_send.at[j],
             recv_sem=n_recv.at[slot],
-            device_id=(d, peer // n_col, peer % n_col),
+            device_id=(d, r, peer),
+            device_id_type=MESH,
+        )
+
+    def row_copy(j, peer, slot):
+        return pltpu.make_async_remote_copy(
+            src_ref=nbuf.at[n_col + slot],
+            dst_ref=nbuf.at[n_col + slot],
+            send_sem=n_send.at[n_col + j],
+            recv_sem=n_recv.at[n_col + slot],
+            device_id=(d, peer, c),
             device_id_type=MESH,
         )
 
@@ -257,18 +265,29 @@
             part = jnp.sum(own * own) + (d == 0).astype(jnp.float32) * (
                 jnp.sum(lg * lg) / float(n_row)
             )
-            nbuf[me_rc] = jnp.full(nbuf.shape[1:], part, jnp.float32)
-            for j in range(1, n_rc):
-                copy = n_copy(j, lax.rem(me_rc + j, n_rc), me_rc)
+            nbuf[c] = jnp.full(nbuf.shape[1:], part, jnp.float32)
+            for j in range(1, n_col):
+                copy = col_copy(j, lax.rem(c + j, n_col), c)
                 copy.start()
                 n_copies.append(copy)
 
-    for j in range(1, n_rc):
-        sender = lax.rem(me_rc + n_rc - j, n_rc)
-        n_copy(j, sender, sender).wait_recv()
+    for j in range(1, n_col):
+        sender = lax.rem(c + n_col - j, n_col)
+        col_copy(j, sender, sender).wait_recv()
     for copy in n_copies:
         copy.wait_send()
-    pbuf[d] = jnp.sum(nbuf[...], axis=0)
+    nbuf[n_col + r] = jnp.sum(nbuf[0:n_col], axis=0)
+    n_copies = []
+    for j in range(1, n_row):
+        copy = row_copy(j, lax.rem(r + j, n_row), r)
+        copy.start()
+        n_copies.append(copy)
+    for j in range(1, n_row):
+        sender = lax.rem(r + n_row - j, n_row)
+        row_copy(j, sender, sender).wait_recv()
+    for copy in n_copies:
+        copy.wait_send()
+    pbuf[d] = jnp.sum(nbuf[n_col:n_col + n_row], axis=0)
     p_copies = []
     for j in range(1, n_dp):
         copy = p_copy(j, lax.rem(d + j, n_dp), d)

time: 73.9 us -> 77.1 us (1.043)
  the two profiles are of different devices: /device:TPU:8 before, /device:TPU:1 now
where the time goes in v16:
time: 77.1 us; the launch traced here: 76.5 us
  Pallas kernels  75.9 us (98%)
    pallas_call x1, Pallas kernels, reduce_blocks(): pl.pallas_call(functools.partial(reduce_kernel, n_dp, n_row, n_col), out_...  71.7 us
    pallas_call x1, Pallas kernels, apply_update(): pl.pallas_call(apply_kernel, out_shape=tuple((jax.ShapeDtypeStruct(x.shap...  4.15 us

profile of v16, /device:TPU:1, one launch (start us, length us, event | category | flops | bytes accessed | tf_op | source)
XLA Modules:
  0.0 76.5 jit_solution(5574570893385829122)
XLA Ops:
  0.6 71.7 %shard_map.161 = (f32[128,1024]{1,0:T(8,128)}, f32[4,256]{1,0:T(4,128)}, f32[8,128]{1,0:T(8,128)}, f32[512,256]{1,0:T(8,128)}) custom-call(bf16[512,256]{1,0:T(8,128)(2,1)} %bitcast.2, bf16[4,256]{1,0:T(4,128)(2,1)} %bitcast.3, f32[128,1024]{1,0:T(8,128)} %m_ref.3, f32[128,1024]{1,0:T(8,128)} %f_ref.3, f32[128,1024]{1,0:T(8,128)} %s_ref.3), custom_call_target="tpu_custom_call" | custom-call | tf_op jit(solution)/shard_map/pallas_call | solution.py:326
  72.3 4.2 %shard_map.162 = (f32[512,256]{1,0:T(8,128)}, f32[128,1024]{1,0:T(8,128)}, f32[128,1024]{1,0:T(8,128)}, f32[128,1024]{1,0:T(8,128)}, f32[4,256]{1,0:T(4,128)}, /...) custom-call(f32[8,128]{1,0:T(8,128)} %get-tuple-element.12.c_ref, f32[128,1024]{1,0:T(8,128)} %get-tuple-element.13.g_ref, ...), custom_call_target="tpu_custom_call" | custom-call | tf_op jit(solution)/shard_map/pallas_call | solution.py:402

commit v17 on v12

--- a/solution.py
+++ b/solution.py
@@ -237,17 +237,18 @@
     sends = []
     waited = set()
     n_copies = []
+    turn = 1 - 2 * (r % 2)
     for leg in range(0, n_right, reach):
         for sign, span in ((1, n_right), (-1, n_left)):
             if leg >= span:
                 continue
             back = (n_dp - sign * leg) % n_dp
-            slot = lax.rem(d + back, n_dp)
+            slot = lax.rem(d + n_dp - sign * leg * turn, n_dp)
             if leg:
                 arrive(slot)
                 waited.add(back)
             for hop in range(1, min(reach, span - leg) + 1):
-                peer = lax.rem(d + (n_dp + sign * hop) % n_dp, n_dp)
+                peer = lax.rem(d + n_dp + sign * hop * turn, n_dp)
                 copy = ag_copy(slot, len(sends), peer)
                 copy.start()
                 sends.append(copy)

time: 73.9 us -> 73.6 us (level)
  no operation moved by 1% of the time
where the time goes in v17:
time: 73.6 us; the launch traced here: 73.5 us
  Pallas kernels  72.8 us (99%)
    pallas_call x1, Pallas kernels, reduce_blocks(): pl.pallas_call(functools.partial(reduce_kernel, n_dp, n_row, n_col), out_...  68.7 us
    pallas_call x1, Pallas kernels, apply_update(): pl.pallas_call(apply_kernel, out_shape=tuple((jax.ShapeDtypeStruct(x.shap...  4.15 us

profile of v17, /device:TPU:8, one launch (start us, length us, event | category | flops | bytes accessed | tf_op | source)
XLA Modules:
  0.0 73.5 jit_solution(10920057094252588261)
XLA Ops:
  0.6 68.7 %shard_map.161 = (f32[128,1024]{1,0:T(8,128)}, f32[4,256]{1,0:T(4,128)}, f32[8,128]{1,0:T(8,128)}, f32[512,256]{1,0:T(8,128)}) custom-call(bf16[512,256]{1,0:T(8,128)(2,1)} %bitcast.2, bf16[4,256]{1,0:T(4,128)(2,1)} %bitcast.3, f32[128,1024]{1,0:T(8,128)} %m_ref.3, f32[128,1024]{1,0:T(8,128)} %f_ref.3, f32[128,1024]{1,0:T(8,128)} %s_ref.3), custom_call_target="tpu_custom_call" | custom-call | tf_op jit(solution)/shard_map/pallas_call | solution.py:308
  69.3 4.2 %shard_map.162 = (f32[512,256]{1,0:T(8,128)}, f32[128,1024]{1,0:T(8,128)}, f32[128,1024]{1,0:T(8,128)}, f32[128,1024]{1,0:T(8,128)}, f32[4,256]{1,0:T(4,128)}, /...) custom-call(f32[8,128]{1,0:T(8,128)} %get-tuple-element.12.c_ref, f32[128,1024]{1,0:T(8,128)} %get-tuple-element.13.g_ref, ...), custom_call_target="tpu_custom_call" | custom-call | tf_op jit(solution)/shard_map/pallas_call | solution.py:384
